TPU v7x, 512 devices: a whole 4x4x16 slice. The times are simulated.
512 devices in a mesh: front: 8 (over x, core), cube: 64 (over y, z).
Axes of the slice: x: 4, y: 4, z: 16, core: 2. Of those that a mesh axis runs over, the one named last changes fastest.
Arguments:
- front: float32 [8, 4096, 4096], P('front', 'cube'), may hold values from -9 to 9, as said below
- own_tiles: float32 [8, 1024, 128, 128], P('front', 'cube'), may hold values from -6 to 6
- partner_tiles: float32 [8, 1024, 128, 128], P('front', 'cube'), may hold values from -6 to 6
- tile_rows: int32 [8, 64, 32, 1], replicated, may hold values from 4 to 31, as said below
- tile_cols: int32 [8, 64, 32], replicated, may hold values from 4 to 31
- live: int32 [8, 64, 2], replicated, may hold values from 8 to 16
Outputs:
- factored: float32 [8, 4096, 4096], P('front', 'cube')
Inputs may be any that keep to these rules, and one draw needn't show every extreme that they name: `front`: Symmetric. Its leading 4 * 128 rows and columns form a strictly diagonally dominant block with diagonal entries in 1.2 to 2.5 and off-diagonal entries of magnitude below 1 / 512. `tile_rows`: within the 16 slots of one child on one device for one parent front the tile rows are distinct, dead slots included; over both children's 2 * 16 slots no tile row is named more than 2 times, and in some device's list one is named exactly 2 times.
All inputs are finite; a program needn't handle non-finite values.
Results may differ from a plain program's by a relative error of at most 0.0001.
Values sent between devices are 32-bit elements; how exact they have to be, the bound alone decides.
A program may use at most 64 MiB of HBM per device.

v0:
```python
import jax
import jax.numpy as jnp
from jax import lax
from jax.sharding import PartitionSpec as P

PANELS = 4
CAP = 2


def swapped(value, axis, apart):
    mask = 2**apart
    pairs = [(source, source ^ mask) for source in range(lax.axis_size(axis))]
    return lax.ppermute(value, axis, pairs)


def route_plan(rows_block, cols_block, tile_size, half_size, rows_dev, tile_count):
    cube_count, count = rows_block.shape
    global_row = rows_block[:, :, None] * tile_size + jnp.arange(2)[None, None, :] * half_size
    global_row = global_row.reshape(cube_count, 2 * count)
    target_dev = global_row // rows_dev
    row_block = global_row % rows_dev // half_size
    piece_cols = jnp.broadcast_to(cols_block[:, :, None], (cube_count, count, 2)).reshape(
        cube_count, 2 * count
    )
    order_pos = jnp.arange(2 * count)
    earlier = order_pos[None, :] < order_pos[:, None]
    same_dest = target_dev[:, :, None] == target_dev[:, None, :]
    slot_rank = jnp.sum(same_dest & earlier[None], axis=2)
    cell_of = row_block * tile_count + piece_cols
    return (target_dev, slot_rank, cell_of)


def pack_sends(holdings, target_dev, slot_rank, position, slot_count, half_size, tile_size):
    cube_count = target_dev.shape[0]
    send_index = lax.dynamic_index_in_dim(target_dev, position, 0, keepdims=False) * slot_count
    send_index = send_index + lax.dynamic_index_in_dim(slot_rank, position, 0, keepdims=False)
    outgoing = jnp.zeros((cube_count * slot_count, half_size, tile_size), jnp.float32)
    outgoing = outgoing.at[send_index].add(holdings.reshape(-1, half_size, tile_size))
    return outgoing.reshape(cube_count, slot_count, half_size, tile_size)


def place_received(
    incoming,
    target_dev,
    slot_rank,
    cell_of,
    position,
    slot_count,
    rows_dev,
    tile_count,
    half_size,
    tile_size,
):
    cube_count = target_dev.shape[0]
    grid_cells = rows_dev // half_size * tile_count
    recv_pos = jnp.arange(cube_count)[:, None] * slot_count + slot_rank
    recv_pos = jnp.where(target_dev == position, recv_pos, cube_count * slot_count)
    placement = jnp.full((cube_count * slot_count,), grid_cells, jnp.int32)
    placement = placement.at[recv_pos.reshape(-1)].set(cell_of.reshape(-1), mode="drop")
    assembled = jnp.zeros((grid_cells, half_size, tile_size), jnp.float32)
    assembled = assembled.at[placement].add(incoming.reshape(-1, half_size, tile_size), mode="drop")
    assembled = assembled.reshape(rows_dev // half_size, tile_count, half_size, tile_size)
    return assembled.transpose(0, 2, 1, 3).reshape(rows_dev, tile_count * tile_size)


def body(front, own_tiles, partner_tiles, tile_rows, tile_cols, live):
    position = lax.axis_index("cube")
    front_pos = lax.axis_index("front")
    rows_dev = front.shape[1]
    order_size = front.shape[2]
    tile_size = own_tiles.shape[-1]
    half_size = tile_size // 2
    tile_count = order_size // tile_size
    per_device = own_tiles.shape[1]
    slot_count = CAP * rows_dev // half_size
    within = jnp.arange(per_device)
    rows_here = lax.dynamic_index_in_dim(tile_rows, front_pos, 0, keepdims=False)[:, :, 0]
    cols_here = lax.dynamic_index_in_dim(tile_cols, front_pos, 0, keepdims=False)
    live_here = lax.dynamic_index_in_dim(live, front_pos, 0, keepdims=False)
    live_mine = lax.dynamic_index_in_dim(live_here, position, 0, keepdims=False)
    arrived = swapped(partner_tiles, "front", 0)
    keep_own = (within < live_mine[0]).astype(jnp.float32)
    keep_arrived = (within < live_mine[1]).astype(jnp.float32)
    holdings = jnp.concatenate(
        [own_tiles[0] * keep_own[:, None, None], arrived[0] * keep_arrived[:, None, None]], axis=0
    )
    target_dev, slot_rank, cell_of = route_plan(
        rows_here, cols_here, tile_size, half_size, rows_dev, tile_count
    )
    outgoing = pack_sends(
        holdings, target_dev, slot_rank, position, slot_count, half_size, tile_size
    )
    incoming = lax.all_to_all(outgoing, "cube", split_axis=0, concat_axis=0, tiled=True)
    added = place_received(
        incoming,
        target_dev,
        slot_rank,
        cell_of,
        position,
        slot_count,
        rows_dev,
        tile_count,
        half_size,
        tile_size,
    )
    matrix = front[0] + added
    row_global = position * rows_dev + jnp.arange(rows_dev)[:, None]
    for panel_idx in range(PANELS):
        first = panel_idx * tile_size
        panel_loc = matrix[:, first : first + tile_size]
        pick_rows = (row_global == first + jnp.arange(tile_size)[None, :]).astype(jnp.float32)
        gathered = lax.all_gather(panel_loc, "cube", axis=0, tiled=True)
        diag_factor = jnp.linalg.cholesky(gathered[first : first + tile_size])
        all_factor = jax.scipy.linalg.solve_triangular(diag_factor, gathered.T, lower=True).T
        all_rows = jnp.arange(order_size)[:, None]
        masked = jnp.where(all_rows >= first + tile_size, all_factor, jnp.zeros_like(all_factor))
        own_masked = lax.dynamic_slice_in_dim(masked, position * rows_dev, rows_dev, 0)
        matrix = matrix - jnp.dot(own_masked, masked.T, precision=lax.Precision.HIGHEST)
        own_factor = lax.dynamic_slice_in_dim(all_factor, position * rows_dev, rows_dev, 0)
        diag_rows = jnp.dot(pick_rows, diag_factor, precision=lax.Precision.HIGHEST)
        placed = jnp.where(row_global < first + tile_size, diag_rows, own_factor)
        placed = jnp.where(row_global < first, jnp.zeros_like(placed), placed)
        matrix = matrix.at[:, first : first + tile_size].set(placed)
    return matrix[None]


def solution(mesh):
    in_specs = (
        P("front", "cube", None),
        P("front", "cube", None, None),
        P("front", "cube", None, None),
        P(),
        P(),
        P(),
    )
    out_specs = P("front", "cube", None)
    return jax.shard_map(body, mesh=mesh, in_specs=in_specs, out_specs=out_specs, check_vma=False)
```

profile of v0, /device:TPU:6, one launch (start us, length us, event | category | flops | bytes accessed | tf_op | source)
XLA Modules:
  0.0 945.8 jit_solution(594090694926188878)
XLA Ops:
  18.4 9.0 scatter_fusion
  27.4 19.0 %all-to-all-start = ((f32[64,2,64,128]{3,2,1,0:T(8,128)}), f32[64,2,64,128]{3,2,1,0:T(8,128)}, u32[]{:S(2)}, u32[]{:S(2)}) async-start(f32[64,2,64,128]{3,2,1,0:T(8,128)} %bitcast.107), calls=%async_computation | async-start | bytes 8388608 | tf_op jit(solution)/shard_map/all_to_all | solution.py:93
  50.0 15.5 %scatter_custom_fusion = s32[128]{0:T(128)S(1)} fusion(s32[4096]{0:T(1024)S(1)} %bitcast.113, s32[4096]{0:T(1024)S(1)} %fusion.55, s32[]{:T(128)} %constant.238.clone.1), kind=kCustom, calls=%fused_computation.162 | custom fusion | bytes 516 | tf_op jit(solution)/shard_map/scatter | solution.py:59
  65.5 169.8 %all-to-all-done = f32[64,2,64,128]{3,2,1,0:T(8,128)} async-done(((f32[64,2,64,128]{3,2,1,0:T(8,128)}), f32[64,2,64,128]{3,2,1,0:T(8,128)}, u32[]{:S(2)}, u32[]{:S(2)}) %all-to-all-start) | async-done | bytes 4194336 | tf_op jit(solution)/shard_map/all_to_all | solution.py:93
  235.4 13.6 %scatter_fusion.1 = f32[32,64,128]{2,1,0:T(8,128)S(1)} fusion(f32[32,64,128]{2,1,0:T(8,128)S(1)} %broadcast_in_dim.109, s32[128]{0:T(128)S(1)} %compare_select_fusion.6, f32[128,64,128]{2,1,0:T(8,128)} %bitcast.13), kind=kCustom, calls=%fused_computation.2 | custom fusion | flops 1048576 | bytes 12583424 | tf_op jit(solution)/shard_map/scatter-add | solution.py:61
  255.8 133.0 %all-gather.5.cloned.1.call-done = f32[4096,128]{1,0:T(8,128)} async-done(((f32[64,128]{1,0:T(8,128)}), f32[4096,128]{1,0:T(8,128)}) %all-gather.5.cloned.1.call-update) | async-done | bytes 2097168 | tf_op jit(solution)/shard_map/all_gather | solution.py:112
  390.5 11.7 %cholesky.74 = f32[128,128]{1,0:T(8,128)S(1)} custom-call(f32[128,128]{1,0:T(8,128)S(1)} %fusion.28), custom_call_target="Cholesky" | custom-call | tf_op jit(solution)/shard_map/jit(cholesky)/cholesky | solution.py:113
  403.6 9.8 %custom-call.8 = f32[1,128,128]{1,2,0:T(8,128)S(1)} custom-call(f32[1,128,128]{2,1,0:T(8,128)S(1)} %select_bitcast_fusion.3), custom_call_target="InvertDiagBlocksLowerTriangular" | custom-call | tf_op jit(solution)/shard_map/jit(_solve_triangular)/triangular_solve | solution.py:114
  413.4 3.7 broadcast_select_fusion.3
  417.1 3.6 convolution_subtract_fusion.3
  424.1 136.0 %all-gather.7.cloned.1.call-done = f32[4096,128]{1,0:T(8,128)} async-done(((f32[64,128]{1,0:T(8,128)}), f32[4096,128]{1,0:T(8,128)}) %all-gather.7.cloned.1.call-update) | async-done | bytes 2097168 | tf_op jit(solution)/shard_map/all_gather | solution.py:112
  561.9 11.7 %cholesky.85 = f32[128,128]{1,0:T(8,128)S(1)} custom-call(f32[128,128]{1,0:T(8,128)S(1)} %fusion.26), custom_call_target="Cholesky" | custom-call | tf_op jit(solution)/shard_map/jit(cholesky)/cholesky | solution.py:113
  575.0 9.8 %custom-call.9 = f32[1,128,128]{1,2,0:T(8,128)S(1)} custom-call(f32[1,128,128]{2,1,0:T(8,128)S(1)} %select_bitcast_fusion.2), custom_call_target="InvertDiagBlocksLowerTriangular" | custom-call | tf_op jit(solution)/shard_map/jit(_solve_triangular)/triangular_solve | solution.py:114
  584.8 3.6 broadcast_select_fusion.2
  588.4 3.6 convolution_subtract_fusion.2
  596.4 136.2 %all-gather.9.cloned.1.call-done = f32[4096,128]{1,0:T(8,128)} async-done(((f32[64,128]{1,0:T(8,128)}), f32[4096,128]{1,0:T(8,128)}) %all-gather.9.cloned.1.call-update) | async-done | bytes 2097168 | tf_op jit(solution)/shard_map/all_gather | solution.py:112
  734.4 11.7 %cholesky.96 = f32[128,128]{1,0:T(8,128)S(1)} custom-call(f32[128,128]{1,0:T(8,128)S(1)} %fusion.24), custom_call_target="Cholesky" | custom-call | tf_op jit(solution)/shard_map/jit(cholesky)/cholesky | solution.py:113
  747.5 9.8 %custom-call.10 = f32[1,128,128]{1,2,0:T(8,128)S(1)} custom-call(f32[1,128,128]{2,1,0:T(8,128)S(1)} %select_bitcast_fusion.1), custom_call_target="InvertDiagBlocksLowerTriangular" | custom-call | tf_op jit(solution)/shard_map/jit(_solve_triangular)/triangular_solve | solution.py:114
  757.3 3.7 broadcast_select_fusion.1
  761.1 3.6 convolution_subtract_fusion.1
  767.8 136.2 %all-gather.11.cloned.1.call-done = f32[4096,128]{1,0:T(8,128)} async-done(((f32[64,128]{1,0:T(8,128)}), f32[4096,128]{1,0:T(8,128)}) %all-gather.11.cloned.1.call-update) | async-done | bytes 2097168 | tf_op jit(solution)/shard_map/all_gather | solution.py:112
  905.8 11.7 %cholesky.107 = f32[128,128]{1,0:T(8,128)S(1)} custom-call(f32[128,128]{1,0:T(8,128)S(1)} %fusion.22), custom_call_target="Cholesky" | custom-call | tf_op jit(solution)/shard_map/jit(cholesky)/cholesky | solution.py:113
  918.9 9.8 %custom-call.11 = f32[1,128,128]{1,2,0:T(8,128)S(1)} custom-call(f32[1,128,128]{2,1,0:T(8,128)S(1)} %select_bitcast_fusion), custom_call_target="InvertDiagBlocksLowerTriangular" | custom-call | tf_op jit(solution)/shard_map/jit(_solve_triangular)/triangular_solve | solution.py:114
  928.7 3.6 broadcast_select_fusion
  (116 shorter events, 52.3 us)
Async XLA Ops:
  6.5 41.8 %copy-start = (s32[8,64,32]{1,2,0:T(8,128)S(1)}, s32[8,64,32]{1,2,0:T(8,128)}, u32[]{:S(2)}) copy-start(s32[8,64,32]{1,2,0:T(8,128)} %param.21) | copy-start | bytes 196612
  6.5 9.1 collective-permute-start
  27.4 207.9 %all-to-all-start = ((f32[64,2,64,128]{3,2,1,0:T(8,128)}), f32[64,2,64,128]{3,2,1,0:T(8,128)}, u32[]{:S(2)}, u32[]{:S(2)}) async-start(f32[64,2,64,128]{3,2,1,0:T(8,128)} %bitcast.107), calls=%async_computation | async-start | bytes 8388608 | tf_op jit(solution)/shard_map/all_to_all | solution.py:93
  46.4 342.3 %all-gather.5.cloned.1.call-start = ((), (), s32[]{:S(2)}) async-start(), calls=%async_computation.1 | async-start | bytes 2129920 | tf_op jit(solution)/shard_map/all_gather | solution.py:112
  46.9 2.4 copy-start.5
  252.8 1.4 copy-start.3
  254.9 305.2 %all-gather.7.cloned.1.call-start = ((), (), s32[]{:S(2)}) async-start(), calls=%async_computation.2 | async-start | bytes 2129920 | tf_op jit(solution)/shard_map/all_gather | solution.py:112
  413.4 3.7 copy-start.4
  423.0 309.6 %all-gather.9.cloned.1.call-start = ((), (), s32[]{:S(2)}) async-start(), calls=%async_computation.3 | async-start | bytes 2129920 | tf_op jit(solution)/shard_map/all_gather | solution.py:112
  593.5 1.4 copy-start.1
  595.5 308.5 %all-gather.11.cloned.1.call-start = ((), (), s32[]{:S(2)}) async-start(), calls=%async_computation.4 | async-start | bytes 2129920 | tf_op jit(solution)/shard_map/all_gather | solution.py:112
  757.3 3.7 copy-start.2
Sparse Core Ops, SparseCore 0:
  255.0 133.6 all-gather.4
  423.1 136.9 all-gather.6
  595.7 136.9 all-gather.8
  767.0 136.9 all-gather.10
where the time goes:
time: 954 us; the launch traced here: 946 us
  waiting for transfers between devices  711 us (75%)
  other arithmetic  128 us (13%)
  local copies, waits for them, and re-layouts  35.8 us (4%)
  matrix products  35 us (4%)
  starting transfers between devices  21.4 us (2%)
  between operations  13.9 us (1%)
    all_gather x4, waiting for transfers between devices, body(): gathered = lax.all_gather(panel_loc, 'cube', axis=0, tiled=True)  541 us
    all_to_all x1, waiting for transfers between devices, body(): lax.all_to_all(outgoing, 'cube', split_axis=0, concat_axis=0, tiled=True)  170 us
    another operation x12, other arithmetic, body(): diag_factor = jnp.linalg.cholesky(gathered[first:first + tile_size])  49.6 us
    another operation x8, other arithmetic, body(): jax.scipy.linalg.solve_triangular(diag_factor, gathered.T, lower=True)  41.9 us
  transfers between devices with their start and end apart: 6, of which 5 were waited for; matrix products, arithmetic and copies ran while one was open for 3% of the time, Pallas kernels for 0%

commit v1 on v0

--- a/solution.py
+++ b/solution.py
@@ -1,10 +1,15 @@
 import jax
 import jax.numpy as jnp
 from jax import lax
+from jax.experimental import pallas as pl
+from jax.experimental.pallas import tpu as pltpu
 from jax.sharding import PartitionSpec as P
 
 PANELS = 4
 CAP = 2
+NY = 4
+NZ = 16
+HI = lax.Precision.HIGHEST
 
 
 def swapped(value, axis, apart):
@@ -63,6 +68,130 @@
     return assembled.transpose(0, 2, 1, 3).reshape(rows_dev, tile_count * tile_size)
 
 
+def gather_kernel(x_ref, out_ref, own_sem, zr_s, zr_r, zl_s, zl_r, yp_s, yp_r, ym_s, ym_r, fp_s, fp_r, fm_s, fm_r):
+    me = lax.axis_index("cube")
+    y, z = me // NZ, me % NZ
+
+    def dev(yy, zz):
+        return {"cube": yy % NY * NZ + zz % NZ}
+
+    half = x_ref.shape[0] // 2
+    barrier = pltpu.get_barrier_semaphore()
+    for peer in (dev(y, z + 1), dev(y, z + NZ - 1), dev(y + 1, z), dev(y + NY - 1, z)):
+        pl.semaphore_signal(barrier, inc=1, device_id=peer, device_id_type=pl.DeviceIdType.MESH)
+    pl.semaphore_wait(barrier, 4)
+
+    def remote(src, dst, send, recv, to):
+        return pltpu.make_async_remote_copy(
+            src_ref=src, dst_ref=dst, send_sem=send, recv_sem=recv,
+            device_id=to, device_id_type=pl.DeviceIdType.MESH,
+        )
+
+    def slot(yy, zz):
+        return out_ref.at[yy % NY * NZ + zz % NZ]
+
+    def z_of(k):
+        return z if k == 0 else (z + NZ - k if k <= 8 else z + k - 8)
+
+    def right(s):
+        ref = slot(y, z + NZ - s)
+        return remote(ref, ref, zr_s.at[s], zr_r.at[s], dev(y, z + 1))
+
+    def left(s):
+        ref = slot(y, z + s)
+        return remote(ref, ref, zl_s.at[s], zl_r.at[s], dev(y, z + NZ - 1))
+
+    def y_up(k):
+        ref = slot(y, z_of(k))
+        return remote(ref, ref, yp_s.at[k], yp_r.at[k], dev(y + 1, z))
+
+    def y_down(k):
+        ref = slot(y, z_of(k))
+        return remote(ref, ref, ym_s.at[k], ym_r.at[k], dev(y + NY - 1, z))
+
+    def f_up(k):
+        ref = slot(y + NY - 1, z_of(k)).at[pl.ds(0, half)]
+        return remote(ref, ref, fp_s.at[k], fp_r.at[k], dev(y + 1, z))
+
+    def f_down(k):
+        ref = slot(y + 1, z_of(k)).at[pl.ds(half, half)]
+        return remote(ref, ref, fm_s.at[k], fm_r.at[k], dev(y + NY - 1, z))
+
+    own = pltpu.make_async_copy(x_ref, out_ref.at[me], own_sem)
+    own.start()
+    own.wait()
+    right(0).start()
+    left(0).start()
+    y_up(0).start()
+    y_down(0).start()
+
+    def forward(k):
+        y_up(k).wait_recv()
+        f_up(k).start()
+        y_down(k).wait_recv()
+        f_down(k).start()
+
+    order = [0]
+    for s in range(1, 9):
+        right(s - 1).wait_recv()
+        if s < 8:
+            right(s).start()
+        y_up(s).start()
+        y_down(s).start()
+        if s < 8:
+            left(s - 1).wait_recv()
+            if s < 7:
+                left(s).start()
+            y_up(s + 8).start()
+            y_down(s + 8).start()
+        for k in order:
+            forward(k)
+        order = [s] if s == 8 else [s, s + 8]
+    for k in order:
+        forward(k)
+    for k in range(16):
+        f_up(k).wait_recv()
+        f_down(k).wait_recv()
+        y_up(k).wait_send()
+        y_down(k).wait_send()
+        f_up(k).wait_send()
+        f_down(k).wait_send()
+    for s in range(8):
+        right(s).wait_send()
+    for s in range(7):
+        left(s).wait_send()
+
+
+def gather_panels(own):
+    rows, cols = own.shape
+    sem = pltpu.SemaphoreType.DMA
+    return pl.pallas_call(
+        gather_kernel,
+        out_shape=jax.ShapeDtypeStruct((NY * NZ, rows, cols), jnp.float32),
+        in_specs=[pl.BlockSpec(memory_space=pl.ANY)],
+        out_specs=pl.BlockSpec(memory_space=pl.ANY),
+        scratch_shapes=[sem, sem((8,)), sem((8,)), sem((7,)), sem((7,))] + [sem((16,))] * 8,
+        compiler_params=pltpu.CompilerParams(collective_id=0, has_side_effects=True),
+        cost_estimate=pl.CostEstimate(flops=0, bytes_accessed=200_000_000, transcendentals=0),
+    )(own)
+
+
+def factor(lead, tile):
+    order = lead.shape[0]
+    work = jnp.concatenate([lead, jnp.eye(order, dtype=jnp.float32)], axis=1)
+    unit = jnp.eye(tile, dtype=jnp.float32)
+    inverse = []
+    for k in range(order // tile):
+        low = jnp.linalg.cholesky(work[:tile, k * tile:(k + 1) * tile])
+        low_inv = jax.scipy.linalg.solve_triangular(low, unit, lower=True)
+        done = jnp.dot(low_inv, work[:tile], precision=HI)
+        inverse.append(done[:, order:])
+        if k + 1 < order // tile:
+            below = done[:, (k + 1) * tile:order]
+            work = work[tile:] - jnp.dot(below.T, done, precision=HI)
+    return jnp.concatenate(inverse, axis=0)
+
+
 def body(front, own_tiles, partner_tiles, tile_rows, tile_cols, live):
     position = lax.axis_index("cube")
     front_pos = lax.axis_index("front")
@@ -72,6 +201,7 @@
     half_size = tile_size // 2
     tile_count = order_size // tile_size
     per_device = own_tiles.shape[1]
+    lead = PANELS * tile_size
     slot_count = CAP * rows_dev // half_size
     within = jnp.arange(per_device)
     rows_here = lax.dynamic_index_in_dim(tile_rows, front_pos, 0, keepdims=False)[:, :, 0]
@@ -91,6 +221,18 @@
         holdings, target_dev, slot_rank, position, slot_count, half_size, tile_size
     )
     incoming = lax.all_to_all(outgoing, "cube", split_axis=0, concat_axis=0, tiled=True)
+
+    own_panel = front[0, :, :lead]
+    panels = gather_panels(own_panel).reshape(order_size, lead)
+    inverse = factor(panels[:lead], tile_size)
+    row_global = position * rows_dev + jnp.arange(rows_dev)[:, None]
+    col_global = jnp.arange(lead)[None, :]
+    own_factor = jnp.dot(own_panel, inverse.T, precision=HI)
+    own_factor = jnp.where(col_global <= row_global, own_factor, 0.0)
+    earlier = jnp.where(col_global < row_global // tile_size * tile_size, own_factor, 0.0)
+    weights = jnp.dot(earlier, inverse, precision=HI)
+    product = jnp.dot(weights, panels[lead:].T, precision=lax.Precision.HIGH)
+
     added = place_received(
         incoming,
         target_dev,
@@ -103,25 +245,8 @@
         half_size,
         tile_size,
     )
-    matrix = front[0] + added
-    row_global = position * rows_dev + jnp.arange(rows_dev)[:, None]
-    for panel_idx in range(PANELS):
-        first = panel_idx * tile_size
-        panel_loc = matrix[:, first : first + tile_size]
-        pick_rows = (row_global == first + jnp.arange(tile_size)[None, :]).astype(jnp.float32)
-        gathered = lax.all_gather(panel_loc, "cube", axis=0, tiled=True)
-        diag_factor = jnp.linalg.cholesky(gathered[first : first + tile_size])
-        all_factor = jax.scipy.linalg.solve_triangular(diag_factor, gathered.T, lower=True).T
-        all_rows = jnp.arange(order_size)[:, None]
-        masked = jnp.where(all_rows >= first + tile_size, all_factor, jnp.zeros_like(all_factor))
-        own_masked = lax.dynamic_slice_in_dim(masked, position * rows_dev, rows_dev, 0)
-        matrix = matrix - jnp.dot(own_masked, masked.T, precision=lax.Precision.HIGHEST)
-        own_factor = lax.dynamic_slice_in_dim(all_factor, position * rows_dev, rows_dev, 0)
-        diag_rows = jnp.dot(pick_rows, diag_factor, precision=lax.Precision.HIGHEST)
-        placed = jnp.where(row_global < first + tile_size, diag_rows, own_factor)
-        placed = jnp.where(row_global < first, jnp.zeros_like(placed), placed)
-        matrix = matrix.at[:, first : first + tile_size].set(placed)
-    return matrix[None]
+    rest = front[0, :, lead:] - product + added[:, lead:]
+    return jnp.concatenate([own_factor, rest], axis=1)[None]
 
 
 def solution(mesh):

time: 954 us -> 454 us (0.48)
  waiting for transfers between devices: 711 us -> 0.01 us
  Pallas kernels: 0 us -> 252 us
  matrix products: 35 us -> 17.3 us
  between operations: 13.9 us -> 0.84 us
    all_gather x4 -> x0, waiting for transfers between devices: 541 us -> none  [body(): gathered = lax.all_gather(panel_loc, 'cube', axis=0, tiled=True)]
    pallas_call x0 -> x1, Pallas kernels: none -> 252 us  [gather_panels(): pl.pallas_call(gather_kernel, out_shape=jax.ShapeDtypeStruct((NY * NZ, ro...]
    all_to_all x1, waiting for transfers between devices: 170 us -> 0.01 us  [body(): lax.all_to_all(outgoing, 'cube', split_axis=0, concat_axis=0, tiled=True)]
    another operation x4, matrix products: 14.6 us -> 1.14 us  [factor(): low_inv = jax.scipy.linalg.solve_triangular(low, unit, lower=True)]
    dot_general x8 -> x10, matrix products: 20.4 us -> 16.2 us  [the longest x1 6.55 us: body(): product = jnp.dot(weights, panels[lead:].T, precision=lax.Precision.HIGH)]
    another operation x24 -> x20, other arithmetic: 94.8 us -> 91.6 us  [the longest x12 49.7 us: factor(): low = jnp.linalg.cholesky(work[:tile, k * tile:(k + 1) * tile])]
  transfers between devices with their start and end apart: 6 -> 2, of which waited for: 5 -> 0; matrix products, arithmetic and copies ran while one was open for 3% -> 31% of each run, Pallas kernels for 0% -> 56%
where the time goes in v1:
time: 454 us; the launch traced here: 449 us
  Pallas kernels  252 us (56%)
  other arithmetic  122 us (27%)
  local copies, waits for them, and re-layouts  35.1 us (8%)
  starting transfers between devices  21.6 us (5%)
  matrix products  17.3 us (4%)
    pallas_call x1, Pallas kernels, gather_panels(): pl.pallas_call(gather_kernel, out_shape=jax.ShapeDtypeStruct((NY * NZ, ro...  252 us
    another operation x12, other arithmetic, factor(): low = jnp.linalg.cholesky(work[:tile, k * tile:(k + 1) * tile])  49.7 us
    another operation x8, other arithmetic, factor(): low_inv = jax.scipy.linalg.solve_triangular(low, unit, lower=True)  41.9 us
    all_to_all x1, starting transfers between devices, body(): lax.all_to_all(outgoing, 'cube', split_axis=0, concat_axis=0, tiled=True)  19.6 us
    scatter x1, local copies, waits for them, and re-layouts, place_received(): placement.at[recv_pos.reshape(-1)].set(cell_of.reshape(-1), mode='drop')  15.8 us
    scatter-add x1, other arithmetic, place_received(): assembled.at[placement]  13.6 us
  transfers between devices with their start and end apart: 2, of which 0 were waited for; matrix products, arithmetic and copies ran while one was open for 31% of the time, Pallas kernels for 56%

profile of v1, /device:TPU:6, one launch (start us, length us, event | category | flops | bytes accessed | tf_op | source)
XLA Modules:
  0.0 449.2 jit_solution(9140918652540601649)
XLA Ops:
  0.0 2.0 collective-permute-start
  5.8 1.9 convert_reduce_fusion
  7.7 1.4 bitcast_multiply_fusion.1
  9.4 2.5 broadcast_in_dim.49
  11.9 9.0 %scatter_fusion = f32[128,64,128]{2,1,0:T(8,128)} fusion(f32[128,64,128]{2,1,0:T(8,128)} %broadcast_in_dim.49, s32[64]{0:T(128)S(1)} %fusion.50, f32[64,64,128]{2,1,0:T(8,128)S(1)} %bitcast.88), kind=kCustom, calls=%fused_computation.1 | custom fusion | flops 524288 | bytes 6291712 | tf_op jit(solution)/shard_map/scatter-add | solution.py:43
  20.9 19.6 %all-to-all-start = ((f32[64,2,64,128]{3,2,1,0:T(8,128)}), f32[64,2,64,128]{3,2,1,0:T(8,128)}, u32[]{:S(2)}, u32[]{:S(2)}) async-start(f32[64,2,64,128]{3,2,1,0:T(8,128)} %bitcast.87), calls=%async_computation | async-start | bytes 8388608 | tf_op jit(solution)/shard_map/all_to_all | solution.py:223
  42.1 1.6 slice_bitcast_fusion.x_ref
  43.7 252.2 %shard_map.64 = f32[64,64,512]{2,1,0:T(8,128)} custom-call(f32[64,512]{1,0:T(8,128)} %slice_bitcast_fusion.x_ref), custom_call_target="tpu_custom_call" | custom-call | bytes 200000000 | tf_op jit(solution)/shard_map/pallas_call | solution.py:168
  296.0 7.6 %slice.109 = f32[56,64,512]{2,1,0:T(8,128)} slice(f32[64,64,512]{2,1,0:T(8,128)} %shard_map.64), slice={[8:64], [0:64], [0:512]} | slice | bytes 14680064 | tf_op jit(solution)/shard_map/slice | solution.py:234
  305.3 11.7 %cholesky.74 = f32[128,128]{1,0:T(8,128)S(1)} custom-call(f32[128,128]{1,0:T(8,128)S(1)} %fusion.38), custom_call_target="Cholesky" | custom-call | tf_op jit(solution)/shard_map/jit(cholesky)/cholesky | solution.py:185
  318.3 9.8 %custom-call.8 = f32[1,128,128]{1,2,0:T(8,128)S(1)} custom-call(f32[1,128,128]{2,1,0:T(8,128)S(1)} %fusion.26), custom_call_target="InvertDiagBlocksLowerTriangular" | custom-call | tf_op jit(solution)/shard_map/jit(_solve_triangular)/triangular_solve | solution.py:186
  329.2 1.6 fusion.1
  330.8 1.1 copy-done.1
  333.0 11.7 %cholesky.85 = f32[128,128]{1,0:T(8,128)S(1)} custom-call(f32[128,128]{1,0:T(8,128)S(1)} %fusion.36), custom_call_target="Cholesky" | custom-call | tf_op jit(solution)/shard_map/jit(cholesky)/cholesky | solution.py:185
  346.1 9.8 %custom-call.9 = f32[1,128,128]{1,2,0:T(8,128)S(1)} custom-call(f32[1,128,128]{2,1,0:T(8,128)S(1)} %fusion.27), custom_call_target="InvertDiagBlocksLowerTriangular" | custom-call | tf_op jit(solution)/shard_map/jit(_solve_triangular)/triangular_solve | solution.py:186
  356.2 1.6 fusion.7
  359.0 11.9 %cholesky.96 = f32[128,128]{1,0:T(8,128)S(1)} custom-call(f32[128,128]{1,0:T(8,128)S(1)} %fusion.34), custom_call_target="Cholesky" | custom-call | tf_op jit(solution)/shard_map/jit(cholesky)/cholesky | solution.py:185
  372.3 9.8 %custom-call.10 = f32[1,128,128]{1,2,0:T(8,128)S(1)} custom-call(f32[1,128,128]{2,1,0:T(8,128)S(1)} %fusion.28), custom_call_target="InvertDiagBlocksLowerTriangular" | custom-call | tf_op jit(solution)/shard_map/jit(_solve_triangular)/triangular_solve | solution.py:186
  384.1 11.7 %cholesky.107 = f32[128,128]{1,0:T(8,128)S(1)} custom-call(f32[128,128]{1,0:T(8,128)S(1)} %fusion.32), custom_call_target="Cholesky" | custom-call | tf_op jit(solution)/shard_map/jit(cholesky)/cholesky | solution.py:185
  397.2 9.8 %custom-call.11 = f32[1,128,128]{1,2,0:T(8,128)S(1)} custom-call(f32[1,128,128]{2,1,0:T(8,128)S(1)} %fusion.29), custom_call_target="InvertDiagBlocksLowerTriangular" | custom-call | tf_op jit(solution)/shard_map/jit(_solve_triangular)/triangular_solve | solution.py:186
  407.1 15.8 %scatter_custom_fusion = s32[128]{0:T(128)S(1)} fusion(s32[4096]{0:T(1024)S(1)} %bitcast.94, s32[4096]{0:T(1024)S(1)} %fusion.46, s32[]{:T(128)} %constant.140.clone.1), kind=kCustom, calls=%fused_computation.126 | custom fusion | bytes 516 | tf_op jit(solution)/shard_map/scatter | solution.py:64
  423.6 2.0 fusion.2
  426.5 13.6 %scatter_fusion.1 = f32[32,64,128]{2,1,0:T(8,128)S(1)} fusion(f32[32,64,128]{2,1,0:T(8,128)S(1)} %broadcast_in_dim.22, s32[128]{0:T(128)S(1)} %compare_select_fusion.6, f32[128,64,128]{2,1,0:T(8,128)} %bitcast.29), kind=kCustom, calls=%fused_computation.2 | custom fusion | flops 1048576 | bytes 12583424 | tf_op jit(solution)/shard_map/scatter-add | solution.py:66
  441.4 6.5 %fusion = f32[64,3584]{1,0:T(8,128)S(1)} fusion(f32[64,512]{1,0:T(8,128)S(1)} %fusion.4, f32[3584,512]{1,0:T(8,128)} %bitcast.86, f32[64,4096]{1,0:T(8,128)S(1)} %bitcast.90, f32[1,64,4096]{2,1,0:T(8,128)S(1)} %copy-done.3), kind=kOutput, calls=%fused_computation.4 | convolution fusion | flops 705101824 | bytes 10223616 | tf_op jit(solution)/shard_map/dot_general | solution.py:234
  (87 shorter events, 22.1 us)
Async XLA Ops:
  0.0 303.7 %copy-start = (s32[8,64,32]{1,2,0:T(8,128)S(1)}, s32[8,64,32]{1,2,0:T(8,128)}, u32[]{:S(2)}) copy-start(s32[8,64,32]{1,2,0:T(8,128)} %param.13) | copy-start | bytes 196612
  0.0 9.1 %collective-permute-start = (f32[1,16,128,128]{3,2,1,0:T(8,128)}, f32[1,16,128,128]{3,2,1,0:T(8,128)S(1)}, u32[]{:S(2)}, u32[]{:S(2)}) collective-permute-start(f32[1,16,128,128]{3,2,1,0:T(8,128)} %param.11), channel_id=1, source_target_pairs={{0,64},{64,0},{128,192},{192,128},{256,320},{320,256},{384,448},{4... | collective-permute-start | bytes 3145736 | tf_op jit(solution)/shard_map/ppermute | solution.py:18
  20.9 405.5 %all-to-all-start = ((f32[64,2,64,128]{3,2,1,0:T(8,128)}), f32[64,2,64,128]{3,2,1,0:T(8,128)}, u32[]{:S(2)}, u32[]{:S(2)}) async-start(f32[64,2,64,128]{3,2,1,0:T(8,128)} %bitcast.87), calls=%async_computation | async-start | bytes 8388608 | tf_op jit(solution)/shard_map/all_to_all | solution.py:223
  303.6 1.2 slice-start
  330.8 1.2 copy-start.1
  332.0 25.9 %copy-start.2 = (f32[384,1024]{0,1:T(8,128)S(1)}, f32[384,1024]{0,1:T(8,128)}, u32[]{:S(2)}) copy-start(f32[384,1024]{0,1:T(8,128)} %copy-done.1) | copy-start | bytes 4718596
  440.1 1.2 copy-start.3

commit v2 on v0

v2 whole, which is shorter than its diff:
```python
import jax
import jax.numpy as jnp
from jax import lax
from jax.experimental import pallas as pl
from jax.experimental.pallas import tpu as pltpu
from jax.sharding import PartitionSpec as P

PANELS = 4
NY = 4
NZ = 16
CELLS = 28
CHUNKS = 4
WIDE = CELLS // CHUNKS
ROUNDS = 6
HIGH = lax.Precision.HIGH
MESH = pl.DeviceIdType.MESH


def exchange_kernel(
    front_ref, own_ref, partner_ref, pick_ref, cols_ref, x_ref, t_ref,
    tiles, packed, ybuf, rbuf, lbuf, first,
    load_sem, pair_s, pair_r, y_s, y_r, r_s, r_r, l_s, l_r,
    zr_s, zr_r, zl_s, zl_r, yp_s, yp_r, ym_s, ym_r, fp_s, fp_r, fm_s, fm_r,
):
    me = lax.axis_index("cube")
    side = lax.axis_index("front")
    y, z = me // NZ, me % NZ
    lead = x_ref.shape[2]
    rows = x_ref.shape[1]
    slots = own_ref.shape[1]
    none = 2 * slots

    def dev(dy, dz):
        return {"cube": (y + dy) % NY * NZ + (z + dz) % NZ}

    mate = {"front": side + 1 - 2 * (side % 2)}
    right, left = dev(0, 1), dev(0, NZ - 1)
    peers = [right, left, dev(1, 0), dev(2, 0), dev(3, 0), mate]
    barrier = pltpu.get_barrier_semaphore()
    for peer in peers:
        pl.semaphore_signal(barrier, inc=1, device_id=peer, device_id_type=MESH)
    pl.semaphore_wait(barrier, len(peers))

    def remote(src, dst, send, recv, to):
        return pltpu.make_async_remote_copy(
            src_ref=src, dst_ref=dst, send_sem=send, recv_sem=recv, device_id=to, device_id_type=MESH
        )

    pair = remote(partner_ref.at[0], tiles.at[pl.ds(slots, slots)], pair_s, pair_r, mate)
    pair.start()
    own = pltpu.make_async_copy(own_ref.at[0], tiles.at[pl.ds(0, slots)], load_sem.at[0])
    own.start()
    mine = pltpu.make_async_copy(front_ref.at[0, :, pl.ds(0, lead)], x_ref.at[me], load_sem.at[1])
    mine.start()
    tiles[none] = jnp.zeros(tiles.shape[1:], jnp.float32)
    own.wait()
    pair.wait()

    def over_y(far, dy):
        return remote(
            packed.at[far, (y + dy) % NY], ybuf.at[far, dy - 1], y_s.at[far, dy - 1], y_r.at[far, dy - 1], dev(dy, 0)
        )

    order = [8]
    for j in range(1, 9):
        order += [8 - j] + ([8 + j] if j < 8 else [])
    for far in order:
        there = (z + far) % NZ
        top = there % 2 * rows
        for to_y in range(NY):
            for child in range(2):
                index = pick_ref[child, to_y * (NZ // 2) + there // 2]
                packed[far, to_y, child] = tiles[index, pl.ds(pl.multiple_of(top, rows), rows), :]
        for dy in range(1, NY):
            over_y(far, dy).start()

    mine.wait()

    def slot(dy, dz):
        return x_ref.at[(y + dy) % NY * NZ + (z + dz) % NZ]

    def z_of(k):
        return 0 if k == 0 else (NZ - k if k <= 8 else k - 8)

    def x_right(s):
        ref = slot(0, NZ - s)
        return remote(ref, ref, zr_s.at[s], zr_r.at[s], right)

    def x_left(s):
        ref = slot(0, s)
        return remote(ref, ref, zl_s.at[s], zl_r.at[s], left)

    def x_up(k):
        ref = slot(0, z_of(k))
        return remote(ref, ref, yp_s.at[k], yp_r.at[k], dev(1, 0))

    def x_down(k):
        ref = slot(0, z_of(k))
        return remote(ref, ref, ym_s.at[k], ym_r.at[k], dev(3, 0))

    def x_pass_up(k):
        ref = slot(3, z_of(k)).at[pl.ds(0, rows // 2)]
        return remote(ref, ref, fp_s.at[k], fp_r.at[k], dev(1, 0))

    def x_pass_down(k):
        ref = slot(1, z_of(k)).at[pl.ds(rows // 2, rows // 2)]
        return remote(ref, ref, fm_s.at[k], fm_r.at[k], dev(3, 0))

    def x_pass(k):
        x_up(k).wait_recv()
        x_pass_up(k).start()
        x_down(k).wait_recv()
        x_pass_down(k).start()

    def cells(g):
        return pl.ds(g * WIDE, WIDE)

    def go_right(j, g):
        src = first.at[cells(g)] if j == 0 else rbuf.at[j - 1, cells(g)]
        return remote(src, rbuf.at[j, cells(g)], r_s.at[j, g], r_r.at[j, g], right)

    def go_left(j, g):
        src = first.at[cells(g)] if j == 0 else lbuf.at[j - 1, cells(g)]
        return remote(src, lbuf.at[j, cells(g)], l_s.at[j, g], l_r.at[j, g], left)

    def wait_y(far):
        for dy in range(1, NY):
            over_y(far, dy).wait_recv()

    def columns(far):
        there = (z + far) % NZ
        return [[cols_ref[there // 2, (y + NY - dy) % NY, child] for child in range(2)] for dy in range(NY)]

    def items(total, cols, far, cell):
        for dy in range(NY):
            for child in range(2):
                share = (cols[dy][child] == cell).astype(jnp.float32)
                tile = packed[far, y, child] if dy == 0 else ybuf[far, dy - 1, child]
                total = total + share * tile
        return total

    def merge(buf, fresh, cols, far, g):
        def one(n, carry):
            cell = g * WIDE + n
            start = jnp.zeros(buf.shape[1:], jnp.float32) if fresh else buf[cell]
            buf[cell] = items(start, cols, far, cell)
            return carry

        lax.fori_loop(0, WIDE, one, 0)

    half_chunks = CHUNKS // 2
    x_right(0).start()
    x_left(0).start()
    wait_y(8)
    cols = columns(8)
    for g in range(CHUNKS):
        merge(first, True, cols, 8, g)
        (go_right(0, g) if g < half_chunks else go_left(0, g)).start()
    x_up(0).start()
    x_down(0).start()

    behind = [0]
    for j in range(1, 9):
        far_r, far_l = 8 - j, (8 + j) % NZ
        wait_y(far_r)
        if j < 8:
            wait_y(far_l)
            cols_r, cols_l = columns(far_r), columns(far_l)
            for g in range(CHUNKS):
                fresh = j == 1 and g >= half_chunks
                if not fresh:
                    go_right(j - 1, g).wait_recv()
                merge(rbuf.at[j - 1], fresh, cols_r, far_r, g)
                go_right(j, g).start()
                fresh = j == 1 and g < half_chunks
                if not fresh:
                    go_left(j - 1, g).wait_recv()
                merge(lbuf.at[j - 1], fresh, cols_l, far_l, g)
                go_left(j, g).start()
        x_right(j - 1).wait_recv()
        if j < 8:
            x_right(j).start()
            x_left(j - 1).wait_recv()
            if j < 7:
                x_left(j).start()
        x_up(j).start()
        x_down(j).start()
        if j < 8:
            x_up(j + 8).start()
            x_down(j + 8).start()
        for k in behind:
            x_pass(k)
        behind = [j] if j == 8 else [j, j + 8]

    cols = columns(0)
    for g in range(CHUNKS):
        go_right(7, g).wait_recv()
        go_left(7, g).wait_recv()
        for n in range(WIDE):
            cell = g * WIDE + n
            t_ref[:, cell * 128:(cell + 1) * 128] = items(rbuf[7, cell] + lbuf[7, cell], cols, 0, cell)
    for k in behind:
        x_pass(k)

    for k in range(NZ):
        x_pass_up(k).wait_recv()
        x_pass_down(k).wait_recv()
        for copy in (x_up(k), x_down(k), x_pass_up(k), x_pass_down(k)):
            copy.wait_send()
        for dy in range(1, NY):
            over_y(k, dy).wait_send()
    for s in range(8):
        x_right(s).wait_send()
        if s < 7:
            x_left(s).wait_send()
    for j in range(8):
        for g in range(CHUNKS):
            if j > 0 or g < half_chunks:
                go_right(j, g).wait_send()
            if j > 0 or g >= half_chunks:
                go_left(j, g).wait_send()


def exchange(front, own_tiles, partner_tiles, pick, cols, lead):
    rows = front.shape[1]
    tile = own_tiles.shape[-1]
    slots = own_tiles.shape[1]
    sem = pltpu.SemaphoreType.DMA
    any_spec = pl.BlockSpec(memory_space=pl.ANY)
    smem = pl.BlockSpec(memory_space=pltpu.SMEM)
    f32 = jnp.float32
    return pl.pallas_call(
        exchange_kernel,
        out_shape=(
            jax.ShapeDtypeStruct((NY * NZ, rows, lead), f32),
            jax.ShapeDtypeStruct((rows, CELLS * tile), f32),
        ),
        in_specs=[any_spec, any_spec, any_spec, smem, smem],
        out_specs=(any_spec, pl.BlockSpec(memory_space=pltpu.VMEM)),
        scratch_shapes=[
            pltpu.VMEM((2 * slots + 1, tile, tile), f32),
            pltpu.VMEM((NZ, NY, 2, rows, tile), f32),
            pltpu.VMEM((NZ, NY - 1, 2, rows, tile), f32),
            pltpu.VMEM((8, CELLS, rows, tile), f32),
            pltpu.VMEM((8, CELLS, rows, tile), f32),
            pltpu.VMEM((CELLS, rows, tile), f32),
            sem((2,)), sem, sem,
            sem((NZ, NY - 1)), sem((NZ, NY - 1)),
            sem((8, CHUNKS)), sem((8, CHUNKS)), sem((8, CHUNKS)), sem((8, CHUNKS)),
            sem((8,)), sem((8,)), sem((7,)), sem((7,)),
        ] + [sem((NZ,))] * 8,
        compiler_params=pltpu.CompilerParams(
            collective_id=0, has_side_effects=True, vmem_limit_bytes=48 * 2**20
        ),
    )(front, own_tiles, partner_tiles, pick, cols)


def factor(lead):
    order = lead.shape[0]
    row = lax.broadcasted_iota(jnp.int32, (order, order), 0)
    col = lax.broadcasted_iota(jnp.int32, (order, order), 1)
    unit = (row == col).astype(jnp.float32)
    keep = jnp.where(row > col, 1.0, jnp.where(row == col, 0.5, 0.0))
    scale = lax.rsqrt(jnp.sum(lead * unit, axis=1))
    gap = lead * scale[:, None] * scale[None, :] - unit
    inverse = (unit - keep * gap) * scale[None, :]
    for _ in range(ROUNDS - 1):
        gap = jnp.dot(jnp.dot(inverse, lead, precision=HIGH), inverse.T, precision=HIGH) - unit
        inverse = inverse - jnp.dot(keep * gap, inverse, precision=HIGH)
    return inverse


def body(front, own_tiles, partner_tiles, tile_rows, tile_cols, live):
    position = lax.axis_index("cube")
    front_pos = lax.axis_index("front")
    rows_dev = front.shape[1]
    order_size = front.shape[2]
    tile = own_tiles.shape[-1]
    slots = own_tiles.shape[1]
    tile_count = order_size // tile
    lead = PANELS * tile
    y, z = position // NZ, position % NZ

    rows_here = lax.dynamic_index_in_dim(tile_rows, front_pos, 0, keepdims=False)[:, :, 0]
    cols_here = lax.dynamic_index_in_dim(tile_cols, front_pos, 0, keepdims=False)
    live_here = lax.dynamic_index_in_dim(live, front_pos, 0, keepdims=False)
    within = jnp.arange(slots)
    rows_z = lax.dynamic_slice_in_dim(rows_here.reshape(NY, NZ, 2, slots), z, 1, 1)[:, 0]
    cols_z = lax.dynamic_slice_in_dim(cols_here.reshape(NY, NZ, 2, slots), z, 1, 1)[:, 0]
    live_z = lax.dynamic_slice_in_dim(live_here.reshape(NY, NZ, 2), z, 1, 1)[:, 0]
    rows_z = jnp.where(within < live_z[:, :, None], rows_z, -1)
    rows_mine = lax.dynamic_index_in_dim(rows_z, y, 0, keepdims=False)
    hit = rows_mine[:, :, None] == jnp.arange(tile_count)
    spot = within[None, :] + slots * jnp.arange(2)[:, None] - 2 * slots
    pick = jnp.sum(jnp.where(hit, spot[:, :, None], 0), axis=1) + 2 * slots
    hit = rows_z[None] == (y * (NZ // 2) + jnp.arange(NZ // 2))[:, None, None, None]
    cols = jnp.sum(jnp.where(hit, cols_z - (PANELS - 1), 0), axis=3) - 1

    panels, added = exchange(front, own_tiles, partner_tiles, pick, cols, lead)
    panels = panels.reshape(order_size, lead)
    own_panel = front[0, :, :lead]
    inverse = factor(panels[:lead])
    row_global = position * rows_dev + jnp.arange(rows_dev)[:, None]
    col_global = jnp.arange(lead)[None, :]
    own_factor = jnp.dot(own_panel, inverse.T, precision=HIGH)
    own_factor = jnp.where(col_global <= row_global, own_factor, 0.0)
    earlier = jnp.where(col_global < row_global // tile * tile, own_factor, 0.0)
    weights = jnp.dot(earlier, inverse, precision=HIGH)
    product = jnp.dot(weights, panels[lead:].T, precision=HIGH)
    rest = front[0, :, lead:] - product + added
    return jnp.concatenate([own_factor, rest], axis=1)[None]


def solution(mesh):
    in_specs = (
        P("front", "cube", None),
        P("front", "cube", None, None),
        P("front", "cube", None, None),
        P(),
        P(),
        P(),
    )
    out_specs = P("front", "cube", None)
    return jax.shard_map(body, mesh=mesh, in_specs=in_specs, out_specs=out_specs, check_vma=False)
```

time: 954 us -> 254 us (0.27)
  waiting for transfers between devices: 711 us -> 0 us
  Pallas kernels: 0 us -> 216 us
  other arithmetic: 128 us -> 4.82 us
  local copies, waits for them, and re-layouts: 35.8 us -> 11.6 us
  starting transfers between devices: 21.4 us -> 0 us
  matrix products: 35 us -> 20.5 us
  between operations: 13.9 us -> 0.27 us
    all_gather x4 -> x0, waiting for transfers between devices: 541 us -> none  [body(): gathered = lax.all_gather(panel_loc, 'cube', axis=0, tiled=True)]
    pallas_call x0 -> x1, Pallas kernels: none -> 216 us  [exchange(): pl.pallas_call(exchange_kernel, out_shape=(jax.ShapeDtypeStruct((NY * NZ,...]
    all_to_all x1 -> x0, waiting for transfers between devices: 170 us -> none  [body(): lax.all_to_all(outgoing, 'cube', split_axis=0, concat_axis=0, tiled=True)]
    another operation x24 -> x0, other arithmetic: 94.8 us -> none  [the longest x12 49.6 us: body(): diag_factor = jnp.linalg.cholesky(gathered[first:first + tile_size])]
    scatter-add x2 -> x0, other arithmetic: 22.6 us -> none  [the longest x1 13.6 us: place_received(): assembled.at[placement]]
    all_to_all x1 -> x0, starting transfers between devices: 19 us -> none  [body(): lax.all_to_all(outgoing, 'cube', split_axis=0, concat_axis=0, tiled=True)]
    scatter x2 -> x0, local copies, waits for them, and re-layouts: 17.1 us -> none  [the longest x1 15.5 us: place_received(): placement.at[recv_pos.reshape(-1)].set(cell_of.reshape(-1), mode='drop')]
    another operation x4 -> x0, matrix products: 14.6 us -> none  [body(): jax.scipy.linalg.solve_triangular(diag_factor, gathered.T, lower=True)]
  transfers between devices with their start and end apart: 6 -> 0, of which waited for: 5 -> 0; matrix products, arithmetic and copies ran while one was open for 3% -> 0% of each run, Pallas kernels for 0% -> 0%
where the time goes in v2:
time: 254 us; the launch traced here: 253 us
  Pallas kernels  216 us (85%)
  matrix products  20.5 us (8%)
  local copies, waits for them, and re-layouts  11.6 us (5%)
  other arithmetic  4.82 us (2%)
    pallas_call x1, Pallas kernels, exchange(): pl.pallas_call(exchange_kernel, out_shape=(jax.ShapeDtypeStruct((NY * NZ,...  216 us
    dot_general x5, matrix products, factor(): jnp.dot(jnp.dot(inverse, lead, precision=HIGH), inverse.T, precision=HIGH)  5.39 us
    dot_general x5, matrix products, factor(): inverse = inverse - jnp.dot(keep * gap, inverse, precision=HIGH)  5.29 us
    dot_general x5, matrix products, factor(): jnp.dot(inverse, lead, precision=HIGH)  5.27 us

profile of v2, /device:TPU:6, one launch (start us, length us, event | category | flops | bytes accessed | tf_op | source)
XLA Modules:
  0.0 252.9 jit_solution(1542486713520452040)
XLA Ops:
  3.9 1.2 copy-done.1
  5.1 1.2 copy-done.3
  6.3 1.2 copy-done.4
  7.5 215.8 %shard_map.64 = (f32[64,64,512]{2,1,0:T(8,128)}, f32[64,3584]{1,0:T(8,128)S(1)}) custom-call(f32[1,64,4096]{2,1,0:T(8,128)S(1)} %copy-done.1, f32[1,16,128,128]{3,2,1,0:T(8,128)S(1)} %copy-done.3, f32[1,16,128,128]{3,2,1,0:T(8,128)S(1)} %copy-done.4, s32[2,32]{1,0:T(2,128)S(1)} %broadcast_add_fusion.2.pick_ref, s32[8,4,2]{2,1,0:T(4,128)S(1)} %broadcast_add_fusion.cols_ref), custom_call_target="tpu_custom_call" | custom-call | tf_op jit(solution)/shard_map/pallas_call | solution.py:232
  223.3 1.5 fusion.28
  224.9 1.7 fusion.8
  226.6 1.0 fusion.29
  227.6 1.2 fusion.1
  228.9 1.3 convolution_subtract_fusion.5
  230.1 1.0 fusion.30
  231.2 1.0 fusion.2
  232.2 1.0 convolution_subtract_fusion.4
  233.2 1.0 fusion.31
  234.2 1.0 fusion.3
  235.3 1.0 convolution_subtract_fusion.3
  236.3 1.2 fusion.32
  237.5 1.0 fusion.4
  238.6 1.0 convolution_subtract_fusion.2
  239.6 1.0 fusion.33
  240.6 1.0 fusion.5
  241.7 1.0 convolution_subtract_fusion.1
  243.8 4.6 %slice.22 = f32[56,64,512]{2,1,0:T(8,128)S(1)} slice(f32[64,64,512]{2,1,0:T(8,128)} %get-tuple-element.7), slice={[8:64], [0:64], [0:512]} | slice | bytes 14680064 | tf_op jit(solution)/shard_map/slice | solution.py:309
  248.4 3.5 %fusion = f32[64,3584]{1,0:T(8,128)S(1)} fusion(f32[64,3584]{1,0:T(8,128)S(1)} %get-tuple-element.8, f32[64,512]{1,0:T(8,128)S(1)} %fusion.14, f32[3584,512]{1,0:T(8,128)S(1)} %bitcast.67, f32[1,64,4096]{2,1,0:T(8,128)S(1)} %copy-done.2), kind=kOutput, calls=%fused_computation.1 | convolution fusion | flops 705101824 | bytes 10223616 | tf_op jit(solution)/shard_map/dot_general | solution.py:309
  251.8 1.0 maximum_bitcast_fusion
  (36 shorter events, 4.9 us)
Async XLA Ops:
  0.0 0.9 copy-start
  3.9 1.2 copy-start.1
  5.1 1.2 copy-start.3
  6.3 1.2 copy-start.4
  237.5 5.2 %copy-start.2 = (f32[1,64,4096]{2,1,0:T(8,128)S(1)}, f32[1,64,4096]{2,1,0:T(8,128)}, u32[]{:S(2)}) copy-start(f32[1,64,4096]{2,1,0:T(8,128)} %front_ref.1) | copy-start | bytes 3145732

commit v3 on v2

v3 whole, which is shorter than its diff:
```python
import jax
import jax.numpy as jnp
from jax import lax
from jax.experimental import pallas as pl
from jax.experimental.pallas import tpu as pltpu
from jax.sharding import PartitionSpec as P

PANELS = 4
NY = 4
NZ = 16
CELLS = 28
CHUNKS = 4
WIDE = CELLS // CHUNKS
ROUNDS = 6
SUB = 128
MESH = pl.DeviceIdType.MESH
NN = (((1,), (0,)), ((), ()))
NT = (((1,), (1,)), ((), ()))


def split(value):
    high = value.astype(jnp.bfloat16)
    return high, (value - high.astype(jnp.float32)).astype(jnp.bfloat16)


def dot3(left, right, dims):
    def dot(a, b):
        return lax.dot_general(a, b, dims, preferred_element_type=jnp.float32)

    return dot(left[0], right[1]) + dot(left[1], right[0]) + dot(left[0], right[0])


def exchange_kernel(
    front_ref, own_ref, partner_ref, pick_ref, cols_ref, out_ref,
    tiles, packed, ybuf, raw1, raw2, raw3, dense, xbuf,
    lead_ref, m_ref, t_ref, g_ref, a_hi, a_lo, m_hi, m_lo, w_hi, w_lo,
    load_sem, pair_s, pair_r, y_s, y_r, raw_s, raw_r, d_s, d_r,
    zr_s, zr_r, zl_s, zl_r, yp_s, yp_r, ym_s, ym_r, fp_s, fp_r, fm_s, fm_r,
):
    me = lax.axis_index("cube")
    side = lax.axis_index("front")
    y, z = me // NZ, me % NZ
    rows, lead = xbuf.shape[1], xbuf.shape[2]
    slots = own_ref.shape[1]
    none = 2 * slots
    tile = tiles.shape[1]

    def dev(dy, dz):
        return {"cube": (y + dy) % NY * NZ + (z + dz) % NZ}

    mate = {"front": side + 1 - 2 * (side % 2)}
    toward = [dev(0, 1), dev(0, NZ - 1)]
    peers = toward + [dev(1, 0), dev(2, 0), dev(3, 0), mate]
    barrier = pltpu.get_barrier_semaphore()
    for peer in peers:
        pl.semaphore_signal(barrier, inc=1, device_id=peer, device_id_type=MESH)
    xbuf[me] = front_ref[0, :, :lead]
    pl.semaphore_wait(barrier, len(peers))

    def remote(src, dst, send, recv, to):
        return pltpu.make_async_remote_copy(
            src_ref=src, dst_ref=dst, send_sem=send, recv_sem=recv, device_id=to, device_id_type=MESH
        )

    pair = remote(partner_ref.at[0], tiles.at[pl.ds(slots, slots)], pair_s, pair_r, mate)
    pair.start()
    own = pltpu.make_async_copy(own_ref.at[0], tiles.at[pl.ds(0, slots)], load_sem)
    own.start()

    def z_abs(k):
        return (z + (0 if k == 0 else (NZ - k if k <= 8 else k - 8))) % NZ

    def slot(dy, zz):
        return xbuf.at[(y + dy) % NY * NZ + zz]

    def x_right(s):
        ref = slot(0, (z + NZ - s) % NZ)
        return remote(ref, ref, zr_s.at[s], zr_r.at[s], toward[0])

    def x_left(s):
        ref = slot(0, (z + s) % NZ)
        return remote(ref, ref, zl_s.at[s], zl_r.at[s], toward[1])

    def x_up(zz):
        ref = slot(0, zz)
        return remote(ref, ref, yp_s.at[zz], yp_r.at[zz], dev(1, 0))

    def x_down(zz):
        ref = slot(0, zz)
        return remote(ref, ref, ym_s.at[zz], ym_r.at[zz], dev(3, 0))

    def x_pass_up(zz):
        ref = slot(3, zz).at[pl.ds(0, rows // 2)]
        return remote(ref, ref, fp_s.at[zz], fp_r.at[zz], dev(1, 0))

    def x_pass_down(zz):
        ref = slot(1, zz).at[pl.ds(rows // 2, rows // 2)]
        return remote(ref, ref, fm_s.at[zz], fm_r.at[zz], dev(3, 0))

    def x_out(k):
        x_up(z_abs(k)).start()
        x_down(z_abs(k)).start()

    def x_pass(k):
        zz = z_abs(k)
        x_up(zz).wait_recv()
        x_pass_up(zz).start()
        x_down(zz).wait_recv()
        x_pass_down(zz).start()

    behind = [0]

    def x_step(s):
        x_right(s - 1).wait_recv()
        if s < 8:
            x_right(s).start()
            x_left(s - 1).wait_recv()
            if s < 7:
                x_left(s).start()
        now = [s] if s == 8 else [s, s + 8]
        for k in now:
            x_out(k)
        for k in behind:
            x_pass(k)
        behind[:] = now

    x_right(0).start()
    x_left(0).start()
    x_out(0)
    tiles[none] = jnp.zeros(tiles.shape[1:], jnp.float32)
    own.wait()
    pair.wait()

    def over_y(far, dy):
        return remote(
            packed.at[far, (y + dy) % NY], ybuf.at[far, pl.ds(2 * dy - 2, 2)],
            y_s.at[far, dy - 1], y_r.at[far, dy - 1], dev(dy, 0),
        )

    def pack(far):
        there = (z + far) % NZ
        top = pl.multiple_of(there % 2 * rows, rows)
        for to_y in range(NY):
            for child in range(2):
                index = pick_ref[child, to_y * (NZ // 2) + there // 2]
                packed[far, to_y, child] = tiles[index, pl.ds(top, rows), :]
        for dy in range(1, NY):
            over_y(far, dy).start()

    def wait_y(far):
        for dy in range(1, NY):
            over_y(far, dy).wait_recv()

    def far_of(way, j):
        return (8 - j if way == 0 else 8 + j) % NZ

    half_list = 4

    def raw_go(way, j):
        far = far_of(way, j)
        to = toward[way]
        dst = (raw1, raw2, raw3)[j]
        mine = packed.at[far, y]
        theirs = ybuf.at[far]
        if j == 0:
            if way == 0:
                pairs = [(mine, pl.ds(0, 2)), (theirs.at[pl.ds(0, 2)], pl.ds(2, 2))]
            else:
                pairs = [(theirs.at[pl.ds(2, 4)], pl.ds(0, 4))]
        else:
            before = (raw1, raw2)[j - 1]
            count = before.shape[1]
            pairs = [(mine, pl.ds(0, 2)), (theirs, pl.ds(2, 6)), (before.at[way], pl.ds(8, count))]
        return [
            remote(a, dst.at[way, b], raw_s.at[way, j, n], raw_r.at[way, j, n], to)
            for n, (a, b) in enumerate(pairs)
        ]

    def cells(g):
        return pl.ds(g * WIDE, WIDE)

    def go(way, j, g):
        return remote(
            dense.at[way, j - 3, cells(g)], dense.at[way, j - 2, cells(g)],
            d_s.at[way, j - 3, g], d_r.at[way, j - 3, g], toward[way],
        )

    def list_cols(far_dest, dz, members):
        there = (z + far_dest) % NZ
        at = (z + dz) % NZ * (NZ // 2) + there // 2
        return [cols_ref[at, (y + NY - dy) % NY * 2 + child] for dy, child in members]

    full = [(dy, child) for dy in range(NY) for child in range(2)]

    def own_items(far):
        cols = list_cols(far, 0, full)
        refs = [packed.at[far, y, c] if dy == 0 else ybuf.at[far, 2 * dy - 2 + c] for dy, c in full]
        return list(zip(cols, refs))

    def raw_items(way, far):
        step = NZ - 1 if way == 0 else 1
        last = full[:half_list] if way == 0 else full[half_list:]
        cols = list_cols(far, step, full) + list_cols(far, 2 * step, full) + list_cols(far, 3 * step, last)
        return [(col, raw3.at[way, n]) for n, col in enumerate(cols)]

    def add(total, items, cell):
        for col, ref in items:
            total = total + (col == cell).astype(jnp.float32) * ref[...]
        return total

    def merge(buf, fresh, items, g):
        def one(n, carry):
            cell = g * WIDE + n
            start = jnp.zeros(buf.shape[1:], jnp.float32) if fresh else buf[cell]
            buf[cell] = add(start, items, cell)
            return carry

        lax.fori_loop(0, WIDE, one, 0)

    def strip(body):
        def one(n, carry):
            body(pl.ds(pl.multiple_of(n * SUB, SUB), SUB), n * SUB)
            return carry

        lax.fori_loop(0, lead // SUB, one, 0)

    def places(start, shape):
        row = lax.broadcasted_iota(jnp.int32, shape, 0) + start
        col = lax.broadcasted_iota(jnp.int32, shape, 1)
        return row, col

    def load_lead():
        for zz in range(8):
            x_pass_up(zz).wait_recv()
            x_pass_down(zz).wait_recv()

        def rows_of(at, start):
            block = xbuf[pl.ds(start // rows, SUB // rows)].reshape(SUB, lead)
            lead_ref[at, :] = block
            a_hi[at, :], a_lo[at, :] = split(block)

        strip(rows_of)

    def keep_m(at, value):
        m_ref[at, :] = value
        m_hi[at, :], m_lo[at, :] = split(value)

    def begin():
        def diagonal(at, start):
            row, col = places(start, (SUB, lead))
            t_ref[at, :] = jnp.where(row == col, lead_ref[at, :], 0.0)

        strip(diagonal)
        across = lax.rsqrt(jnp.sum(t_ref[...], axis=0, keepdims=True))

        def rows_of(at, start):
            row, col = places(start, (SUB, lead))
            down = lax.rsqrt(jnp.sum(t_ref[at, :], axis=1, keepdims=True))
            lower = jnp.where(row > col, lead_ref[at, :] * down, 0.0)
            unit = (row == col).astype(jnp.float32)
            diag = jnp.where(row == col, lead_ref[at, :], 0.0) * down * across
            keep_m(at, (unit - lower * across - 0.5 * (diag - unit)) * across)

        strip(rows_of)

    def round_a():
        def rows_of(at, start):
            t_ref[at, :] = dot3((m_hi[at, :], m_lo[at, :]), (a_hi[...], a_lo[...]), NN)

        strip(rows_of)

    def round_b():
        def rows_of(at, start):
            row, col = places(start, (SUB, lead))
            gap = dot3(split(t_ref[at, :]), (m_hi[...], m_lo[...]), NT)
            g_ref[at, :] = jnp.where(row > col, gap, jnp.where(row == col, 0.5 * (gap - 1.0), 0.0))

        strip(rows_of)

    def round_c():
        def rows_of(at, start):
            t_ref[at, :] = m_ref[at, :] - dot3(split(g_ref[at, :]), (m_hi[...], m_lo[...]), NN)

        strip(rows_of)
        strip(lambda at, start: keep_m(at, t_ref[at, :]))

    def weigh():
        inverse = (m_hi[...], m_lo[...])
        row, col = places(me * rows, (rows, lead))
        value = dot3(split(xbuf[me]), inverse, NT)
        value = jnp.where(col <= row, value, 0.0)
        out_ref[0, :, :lead] = value
        value = jnp.where(col < row // tile * tile, value, 0.0)
        w_hi[...], w_lo[...] = split(dot3(split(value), inverse, NN))

    def rest_panels():
        for zz in range(8, NZ):
            x_pass_up(zz).wait_recv()
            x_pass_down(zz).wait_recv()

    def subtract(g):
        weights = (w_hi[...], w_lo[...])

        def one(n, carry):
            cell = g * WIDE + n
            block = xbuf[pl.ds(lead // rows + tile // rows * cell, tile // rows)].reshape(tile, lead)
            at = pl.ds(pl.multiple_of(lead + cell * tile, tile), tile)
            out_ref[0, :, at] = front_ref[0, :, at] - dot3(weights, split(block), NT)
            return carry

        lax.fori_loop(0, WIDE, one, 0)

    todo = [load_lead, begin]
    for _ in range(ROUNDS - 1):
        todo += [round_a, round_b, round_c]
    todo += [weigh, rest_panels] + [lambda g=g: subtract(g) for g in range(CHUNKS)]

    def work(count):
        for _ in range(count):
            if todo:
                todo.pop(0)()

    for far in (8, 7, 9, 6, 10):
        pack(far)
    x_step(1)
    wait_y(8)
    for way in range(2):
        for copy in raw_go(way, 0):
            copy.start()
    for j in range(1, 3):
        x_step(2 * j)
        for way in range(2):
            wait_y(far_of(way, j))
            for copy in raw_go(way, j - 1):
                copy.wait_recv()
            for copy in raw_go(way, j):
                copy.start()
        pack(far_of(0, j + 2))
        pack(far_of(1, j + 2))
        x_step(2 * j + 1)
    for way in range(2):
        wait_y(far_of(way, 3))
        for copy in raw_go(way, 2):
            copy.wait_recv()
    items = [own_items(far_of(way, 3)) + raw_items(way, far_of(way, 3)) for way in range(2)]
    for g in range(CHUNKS):
        for way in range(2):
            merge(dense.at[way, 0], True, items[way], g)
            go(way, 3, g).start()
    for far in (far_of(0, 5), far_of(1, 5), far_of(0, 6), far_of(1, 6)):
        pack(far)
    x_step(6)
    x_step(7)
    for j in range(4, 8):
        for way in range(2):
            wait_y(far_of(way, j))
        items = [own_items(far_of(way, j)) for way in range(2)]
        for g in range(CHUNKS):
            for way in range(2):
                go(way, j - 1, g).wait_recv()
                merge(dense.at[way, j - 3], False, items[way], g)
                go(way, j, g).start()
            if j > 4:
                work(2)
        if j == 4:
            for far in (far_of(0, 7), far_of(1, 7), 0):
                pack(far)
            x_step(8)
            for k in behind:
                x_pass(k)

    while todo:
        work(1)
    wait_y(0)
    items = own_items(0)
    for g in range(CHUNKS):
        for way in range(2):
            go(way, 7, g).wait_recv()

        def last(n, carry):
            cell = g * WIDE + n
            at = pl.ds(pl.multiple_of(lead + cell * tile, tile), tile)
            total = add(dense[0, 5, cell] + dense[1, 5, cell], items, cell)
            out_ref[0, :, at] = out_ref[0, :, at] + total
            return carry

        lax.fori_loop(0, WIDE, last, 0)

    for zz in range(NZ):
        for copy in (x_up(zz), x_down(zz), x_pass_up(zz), x_pass_down(zz)):
            copy.wait_send()
        for dy in range(1, NY):
            over_y(zz, dy).wait_send()
    for s in range(8):
        x_right(s).wait_send()
        if s < 7:
            x_left(s).wait_send()
    for way in range(2):
        for j in range(3):
            for copy in raw_go(way, j):
                copy.wait_send()
        for j in range(3, 8):
            for g in range(CHUNKS):
                go(way, j, g).wait_send()


def exchange(front, own_tiles, partner_tiles, pick, cols, lead):
    rows = front.shape[1]
    tile = own_tiles.shape[-1]
    slots = own_tiles.shape[1]
    sem = pltpu.SemaphoreType.DMA
    any_spec = pl.BlockSpec(memory_space=pl.ANY)
    smem = pl.BlockSpec(memory_space=pltpu.SMEM)
    vmem = pl.BlockSpec(memory_space=pltpu.VMEM)
    f32, bf16 = jnp.float32, jnp.bfloat16
    return pl.pallas_call(
        exchange_kernel,
        out_shape=jax.ShapeDtypeStruct(front.shape, f32),
        in_specs=[vmem, any_spec, any_spec, smem, smem],
        out_specs=vmem,
        scratch_shapes=[
            pltpu.VMEM((2 * slots + 1, tile, tile), f32),
            pltpu.VMEM((NZ, NY, 2, rows, tile), f32),
            pltpu.VMEM((NZ, 2 * NY - 2, rows, tile), f32),
            pltpu.VMEM((2, 4, rows, tile), f32),
            pltpu.VMEM((2, 12, rows, tile), f32),
            pltpu.VMEM((2, 20, rows, tile), f32),
            pltpu.VMEM((2, 6, CELLS, rows, tile), f32),
            pltpu.VMEM((NY * NZ, rows, lead), f32),
        ]
        + [pltpu.VMEM((lead, lead), f32)] * 4
        + [pltpu.VMEM((lead, lead), bf16)] * 4
        + [pltpu.VMEM((rows, lead), bf16)] * 2
        + [
            sem, sem, sem,
            sem((NZ, NY - 1)), sem((NZ, NY - 1)),
            sem((2, 3, 3)), sem((2, 3, 3)),
            sem((2, 5, CHUNKS)), sem((2, 5, CHUNKS)),
            sem((8,)), sem((8,)), sem((7,)), sem((7,)),
        ] + [sem((NZ,))] * 8,
        compiler_params=pltpu.CompilerParams(
            collective_id=0, has_side_effects=True, vmem_limit_bytes=56 * 2**20
        ),
    )(front, own_tiles, partner_tiles, pick, cols)


def body(front, own_tiles, partner_tiles, tile_rows, tile_cols, live):
    position = lax.axis_index("cube")
    front_pos = lax.axis_index("front")
    tile = own_tiles.shape[-1]
    slots = own_tiles.shape[1]
    tile_count = front.shape[2] // tile
    y, z = position // NZ, position % NZ

    rows_here = lax.dynamic_index_in_dim(tile_rows, front_pos, 0, keepdims=False)[:, :, 0]
    cols_here = lax.dynamic_index_in_dim(tile_cols, front_pos, 0, keepdims=False)
    live_here = lax.dynamic_index_in_dim(live, front_pos, 0, keepdims=False)
    within = jnp.arange(slots)
    rows_here = rows_here.reshape(NY * NZ, 2, slots)
    cols_here = cols_here.reshape(NY * NZ, 2, slots)
    rows_here = jnp.where(within < live_here[:, :, None], rows_here, -1)
    rows_mine = lax.dynamic_index_in_dim(rows_here, position, 0, keepdims=False)
    hit = rows_mine[:, :, None] == jnp.arange(tile_count)
    spot = within[None, :] + slots * jnp.arange(2)[:, None] - 2 * slots
    pick = jnp.sum(jnp.where(hit, spot[:, :, None], 0), axis=1) + 2 * slots
    hit = rows_here[None] == (y * (NZ // 2) + jnp.arange(NZ // 2))[:, None, None, None]
    cols = jnp.sum(jnp.where(hit, cols_here - (PANELS - 1), 0), axis=3) - 1
    cols = cols.reshape(NZ // 2, NY, NZ, 2).transpose(2, 0, 1, 3).reshape(NZ * NZ // 2, 2 * NY)
    return exchange(front, own_tiles, partner_tiles, pick, cols, PANELS * tile)


def solution(mesh):
    in_specs = (
        P("front", "cube", None),
        P("front", "cube", None, None),
        P("front", "cube", None, None),
        P(),
        P(),
        P(),
    )
    out_specs = P("front", "cube", None)
    return jax.shard_map(body, mesh=mesh, in_specs=in_specs, out_specs=out_specs, check_vma=False)
```

time: 254 us -> 198 us (0.78)
  Pallas kernels: 216 us -> 190 us
  matrix products: 20.5 us -> 0 us
  local copies, waits for them, and re-layouts: 11.6 us -> 5.03 us
  other arithmetic: 4.82 us -> 1.62 us
    pallas_call x1, Pallas kernels: 216 us -> 190 us  [exchange(): pl.pallas_call(exchange_kernel, out_shape=jax.ShapeDtypeStruct(front.shap...]
    dot_general x18 -> x0, matrix products: 20.5 us -> none  [the longest x5 5.39 us: factor(): jnp.dot(jnp.dot(inverse, lead, precision=HIGH), inverse.T, precision=HIGH)]
    slice x1 -> x0, local copies, waits for them, and re-layouts: 4.59 us -> none  [body(): product = jnp.dot(weights, panels[lead:].T, precision=HIGH)]
where the time goes in v3:
time: 198 us; the launch traced here: 197 us
  Pallas kernels  190 us (96%)
  local copies, waits for them, and re-layouts  5.03 us (3%)
    pallas_call x1, Pallas kernels, exchange(): pl.pallas_call(exchange_kernel, out_shape=jax.ShapeDtypeStruct(front.shap...  190 us

profile of v3, /device:TPU:6, one launch (start us, length us, event | category | flops | bytes accessed | tf_op | source)
XLA Modules:
  0.0 197.2 jit_solution(14675366668429013238)
XLA Ops:
  0.0 0.0 copy-start
  0.0 0.9 copy-done
  0.9 0.1 add_add_fusion
  1.0 0.7 dynamic-slice_bitcast_fusion
  1.7 0.2 dynamic-slice_reduce_fusion
  1.9 0.1 select_reduce_fusion.1
  2.0 0.6 broadcast_add_fusion.pick_ref
  2.6 0.7 dynamic-slice_add_fusion
  3.3 0.1 select_reduce_fusion
  3.4 0.1 sub.25
  3.5 0.1 copy.25
  3.6 0.1 reshape.54
  3.7 0.7 copy.26.cols_ref
  4.4 190.5 %shard_map.64 = f32[1,64,4096]{2,1,0:T(8,128)} custom-call(f32[1,64,4096]{2,1,0:T(8,128)} %front_ref.1, f32[1,16,128,128]{3,2,1,0:T(8,128)} %own_ref.1, f32[1,16,128,128]{3,2,1,0:T(8,128)} %partner_ref.1, s32[2,32]{1,0:T(2,128)} %broadcast_add_fusion.pick_ref, s32[128,8]{1,0:T(8,128)} %copy.26.cols_ref), custom_call_target="tpu_custom_call" | custom-call | tf_op jit(solution)/shard_map/pallas_call | solution.py:416
  194.9 2.3 %copy.29 = f32[1,64,4096]{2,1,0:T(8,128)} copy(f32[1,64,4096]{2,1,0:T(8,128)} %shard_map.64) | data formatting | bytes 2097152
  (5 shorter events, 0.0 us)
Async XLA Ops:
  0.0 0.9 copy-start

commit v4 on v3

--- a/solution.py
+++ b/solution.py
@@ -67,9 +67,6 @@
     own = pltpu.make_async_copy(own_ref.at[0], tiles.at[pl.ds(0, slots)], load_sem)
     own.start()
 
-    def z_abs(k):
-        return (z + (0 if k == 0 else (NZ - k if k <= 8 else k - 8))) % NZ
-
     def slot(dy, zz):
         return xbuf.at[(y + dy) % NY * NZ + zz]
 
@@ -97,18 +94,15 @@
         ref = slot(1, zz).at[pl.ds(rows // 2, rows // 2)]
         return remote(ref, ref, fm_s.at[zz], fm_r.at[zz], dev(3, 0))
 
-    def x_out(k):
-        x_up(z_abs(k)).start()
-        x_down(z_abs(k)).start()
-
-    def x_pass(k):
-        zz = z_abs(k)
+    def x_out(zz):
+        x_up(zz).start()
+        x_down(zz).start()
+
+    def x_pass(zz):
         x_up(zz).wait_recv()
         x_pass_up(zz).start()
         x_down(zz).wait_recv()
         x_pass_down(zz).start()
-
-    behind = [0]
 
     def x_step(s):
         x_right(s - 1).wait_recv()
@@ -117,16 +111,9 @@
             x_left(s - 1).wait_recv()
             if s < 7:
                 x_left(s).start()
-        now = [s] if s == 8 else [s, s + 8]
-        for k in now:
-            x_out(k)
-        for k in behind:
-            x_pass(k)
-        behind[:] = now
 
     x_right(0).start()
     x_left(0).start()
-    x_out(0)
     tiles[none] = jnp.zeros(tiles.shape[1:], jnp.float32)
     own.wait()
     pair.wait()
@@ -320,37 +307,58 @@
             if todo:
                 todo.pop(0)()
 
-    for far in (8, 7, 9, 6, 10):
+    def raw_start(way, j, own):
+        copies = raw_go(way, j)
+        count = len(copies) if j == 0 else 2
+        for copy in copies[:count] if own else copies[count:]:
+            copy.start()
+
+    def raw_recv(j):
+        for way in range(2):
+            for copy in raw_go(way, j):
+                copy.wait_recv()
+
+    def raw_own(j):
+        for way in range(2):
+            wait_y(far_of(way, j))
+            raw_start(way, j, True)
+
+    def raw_forward(j):
+        raw_recv(j - 1)
+        for way in range(2):
+            raw_start(way, j, False)
+
+    for far in (8, 7, 9, 6, 10, 5, 11):
         pack(far)
     x_step(1)
     wait_y(8)
     for way in range(2):
-        for copy in raw_go(way, 0):
-            copy.start()
-    for j in range(1, 3):
-        x_step(2 * j)
-        for way in range(2):
-            wait_y(far_of(way, j))
-            for copy in raw_go(way, j - 1):
-                copy.wait_recv()
-            for copy in raw_go(way, j):
-                copy.start()
-        pack(far_of(0, j + 2))
-        pack(far_of(1, j + 2))
-        x_step(2 * j + 1)
+        raw_start(way, 0, True)
+    for far in (4, 12, 3, 13, 2, 14, 1, 15, 0):
+        pack(far)
+    x_step(2)
+    raw_own(1)
+    x_step(3)
+    raw_forward(1)
+    x_step(4)
+    raw_own(2)
+    x_step(5)
+    raw_forward(2)
+    x_step(6)
+    raw_recv(2)
     for way in range(2):
         wait_y(far_of(way, 3))
-        for copy in raw_go(way, 2):
-            copy.wait_recv()
     items = [own_items(far_of(way, 3)) + raw_items(way, far_of(way, 3)) for way in range(2)]
     for g in range(CHUNKS):
         for way in range(2):
             merge(dense.at[way, 0], True, items[way], g)
             go(way, 3, g).start()
-    for far in (far_of(0, 5), far_of(1, 5), far_of(0, 6), far_of(1, 6)):
-        pack(far)
-    x_step(6)
-    x_step(7)
+        if g == 1:
+            x_step(7)
+    x_step(8)
+    for zz in range(8):
+        x_out(zz)
+    outs, passes = list(range(8, NZ)), list(range(NZ))
     for j in range(4, 8):
         for way in range(2):
             wait_y(far_of(way, j))
@@ -360,14 +368,16 @@
                 go(way, j - 1, g).wait_recv()
                 merge(dense.at[way, j - 3], False, items[way], g)
                 go(way, j, g).start()
-            if j > 4:
-                work(2)
-        if j == 4:
-            for far in (far_of(0, 7), far_of(1, 7), 0):
-                pack(far)
-            x_step(8)
-            for k in behind:
-                x_pass(k)
+            slot_at = (j - 4) * CHUNKS + g
+            if slot_at > 0:
+                for zz in passes[:2]:
+                    x_pass(zz)
+                del passes[:2]
+                for zz in outs[:2]:
+                    x_out(zz)
+                del outs[:2]
+            if slot_at > 5:
+                work(3)
 
     while todo:
         work(1)

time: 198 us -> 194 us (0.980)
  Pallas kernels: 190 us -> 187 us
    pallas_call x1, Pallas kernels: 190 us -> 187 us  [exchange(): pl.pallas_call(exchange_kernel, out_shape=jax.ShapeDtypeStruct(front.shap...]
where the time goes in v4:
time: 194 us
  Pallas kernels  187 us (96%)
  local copies, waits for them, and re-layouts  5.03 us (3%)
    pallas_call x1, Pallas kernels, exchange(): pl.pallas_call(exchange_kernel, out_shape=jax.ShapeDtypeStruct(front.shap...  187 us

profile of v4, /device:TPU:6, one launch (start us, length us, event | category | flops | bytes accessed | tf_op | source)
XLA Modules:
  0.0 193.7 jit_solution(3510203464054184187)
XLA Ops:
  0.0 0.0 copy-start
  0.0 0.9 copy-done
  0.9 0.1 add_add_fusion
  1.0 0.7 dynamic-slice_bitcast_fusion
  1.7 0.2 dynamic-slice_reduce_fusion
  1.9 0.1 select_reduce_fusion.1
  2.0 0.6 broadcast_add_fusion.pick_ref
  2.6 0.7 dynamic-slice_add_fusion
  3.3 0.1 select_reduce_fusion
  3.4 0.1 sub.25
  3.5 0.1 copy.25
  3.6 0.1 reshape.54
  3.7 0.7 copy.26.cols_ref
  4.4 187.0 %shard_map.64 = f32[1,64,4096]{2,1,0:T(8,128)} custom-call(f32[1,64,4096]{2,1,0:T(8,128)} %front_ref.1, f32[1,16,128,128]{3,2,1,0:T(8,128)} %own_ref.1, f32[1,16,128,128]{3,2,1,0:T(8,128)} %partner_ref.1, s32[2,32]{1,0:T(2,128)} %broadcast_add_fusion.pick_ref, s32[128,8]{1,0:T(8,128)} %copy.26.cols_ref), custom_call_target="tpu_custom_call" | custom-call | tf_op jit(solution)/shard_map/pallas_call | solution.py:426
  191.4 2.3 %copy.29 = f32[1,64,4096]{2,1,0:T(8,128)} copy(f32[1,64,4096]{2,1,0:T(8,128)} %shard_map.64) | data formatting | bytes 2097152
  (5 shorter events, 0.0 us)
Async XLA Ops:
  0.0 0.9 copy-start

commit v5 on v4

--- a/solution.py
+++ b/solution.py
@@ -12,6 +12,7 @@
 CHUNKS = 4
 WIDE = CELLS // CHUNKS
 ROUNDS = 6
+COARSE = 2
 SUB = 128
 MESH = pl.DeviceIdType.MESH
 NN = (((1,), (0,)), ((), ()))
@@ -23,11 +24,13 @@
     return high, (value - high.astype(jnp.float32)).astype(jnp.bfloat16)
 
 
+def dot1(left, right, dims):
+    return lax.dot_general(left, right, dims, preferred_element_type=jnp.float32)
+
+
 def dot3(left, right, dims):
-    def dot(a, b):
-        return lax.dot_general(a, b, dims, preferred_element_type=jnp.float32)
-
-    return dot(left[0], right[1]) + dot(left[1], right[0]) + dot(left[0], right[0])
+    small = dot1(left[0], right[1], dims) + dot1(left[1], right[0], dims)
+    return small + dot1(left[0], right[0], dims)
 
 
 def exchange_kernel(
@@ -250,26 +253,47 @@
 
         strip(rows_of)
 
-    def round_a():
-        def rows_of(at, start):
-            t_ref[at, :] = dot3((m_hi[at, :], m_lo[at, :]), (a_hi[...], a_lo[...]), NN)
-
-        strip(rows_of)
-
-    def round_b():
-        def rows_of(at, start):
-            row, col = places(start, (SUB, lead))
-            gap = dot3(split(t_ref[at, :]), (m_hi[...], m_lo[...]), NT)
-            g_ref[at, :] = jnp.where(row > col, gap, jnp.where(row == col, 0.5 * (gap - 1.0), 0.0))
-
-        strip(rows_of)
-
-    def round_c():
-        def rows_of(at, start):
-            t_ref[at, :] = m_ref[at, :] - dot3(split(g_ref[at, :]), (m_hi[...], m_lo[...]), NN)
-
-        strip(rows_of)
-        strip(lambda at, start: keep_m(at, t_ref[at, :]))
+    def round_of(exact):
+        def pair(high, low):
+            return (high, low) if exact else (high,)
+
+        def product(left, right, dims):
+            return dot3(left, right, dims) if exact else dot1(left[0], right[0], dims)
+
+        def each(body):
+            for n in range(lead // SUB):
+                body(pl.ds(n * SUB, SUB), pl.ds(0, (n + 1) * SUB), n * SUB)
+
+        def round_a():
+            def rows_of(at, upto, start):
+                left = pair(m_hi[at, upto], m_lo[at, upto])
+                t_ref[at, upto] = product(left, pair(a_hi[upto, upto], a_lo[upto, upto]), NN)
+
+            each(rows_of)
+
+        def round_b():
+            def rows_of(at, upto, start):
+                gap = product(split(t_ref[at, upto]), pair(m_hi[upto, upto], m_lo[upto, upto]), NT)
+                row, col = places(start, gap.shape)
+                g_ref[at, upto] = jnp.where(row > col, gap, jnp.where(row == col, 0.5 * (gap - 1.0), 0.0))
+
+            each(rows_of)
+
+        def round_c():
+            def rows_of(at, upto, start):
+                fix = product(split(g_ref[at, upto]), pair(m_hi[upto, upto], m_lo[upto, upto]), NN)
+                t_ref[at, upto] = m_ref[at, upto] - fix
+
+            each(rows_of)
+
+            def keep(at, upto, start):
+                value = t_ref[at, upto]
+                m_ref[at, upto] = value
+                m_hi[at, upto], m_lo[at, upto] = split(value)
+
+            each(keep)
+
+        return [round_a, round_b, round_c]
 
     def weigh():
         inverse = (m_hi[...], m_lo[...])
@@ -298,8 +322,8 @@
         lax.fori_loop(0, WIDE, one, 0)
 
     todo = [load_lead, begin]
-    for _ in range(ROUNDS - 1):
-        todo += [round_a, round_b, round_c]
+    for n in range(1, ROUNDS):
+        todo += round_of(n > COARSE)
     todo += [weigh, rest_panels] + [lambda g=g: subtract(g) for g in range(CHUNKS)]
 
     def work(count):
@@ -377,7 +401,7 @@
                     x_out(zz)
                 del outs[:2]
             if slot_at > 5:
-                work(3)
+                work(2 if slot_at < 12 else 3)
 
     while todo:
         work(1)

time: 194 us -> 182 us (0.938)
  Pallas kernels: 187 us -> 174 us
    pallas_call x1, Pallas kernels: 187 us -> 174 us  [exchange(): pl.pallas_call(exchange_kernel, out_shape=jax.ShapeDtypeStruct(front.shap...]
where the time goes in v5:
time: 182 us; the launch traced here: 181 us
  Pallas kernels  174 us (96%)
  local copies, waits for them, and re-layouts  5.03 us (3%)
    pallas_call x1, Pallas kernels, exchange(): pl.pallas_call(exchange_kernel, out_shape=jax.ShapeDtypeStruct(front.shap...  174 us

profile of v5, /device:TPU:6, one launch (start us, length us, event | category | flops | bytes accessed | tf_op | source)
XLA Modules:
  0.0 180.9 jit_solution(11810502029585105025)
XLA Ops:
  0.0 0.0 copy-start
  0.0 0.9 copy-done
  0.9 0.1 add_add_fusion
  1.0 0.7 dynamic-slice_bitcast_fusion
  1.7 0.2 dynamic-slice_reduce_fusion
  1.9 0.1 select_reduce_fusion.1
  2.0 0.6 broadcast_add_fusion.pick_ref
  2.6 0.7 dynamic-slice_add_fusion
  3.3 0.1 select_reduce_fusion
  3.4 0.1 sub.25
  3.5 0.1 copy.25
  3.6 0.1 reshape.54
  3.7 0.7 copy.26.cols_ref
  4.4 174.2 %shard_map.64 = f32[1,64,4096]{2,1,0:T(8,128)} custom-call(f32[1,64,4096]{2,1,0:T(8,128)} %front_ref.1, f32[1,16,128,128]{3,2,1,0:T(8,128)} %own_ref.1, f32[1,16,128,128]{3,2,1,0:T(8,128)} %partner_ref.1, s32[2,32]{1,0:T(2,128)} %broadcast_add_fusion.pick_ref, s32[128,8]{1,0:T(8,128)} %copy.26.cols_ref), custom_call_target="tpu_custom_call" | custom-call | tf_op jit(solution)/shard_map/pallas_call | solution.py:450
  178.7 2.3 %copy.29 = f32[1,64,4096]{2,1,0:T(8,128)} copy(f32[1,64,4096]{2,1,0:T(8,128)} %shard_map.64) | data formatting | bytes 2097152
  (5 shorter events, 0.0 us)
Async XLA Ops:
  0.0 0.9 copy-start

commit v6 on v5

--- a/solution.py
+++ b/solution.py
@@ -57,7 +57,10 @@
     barrier = pltpu.get_barrier_semaphore()
     for peer in peers:
         pl.semaphore_signal(barrier, inc=1, device_id=peer, device_id_type=MESH)
-    xbuf[me] = front_ref[0, :, :lead]
+    mine = pltpu.make_async_copy(front_ref.at[0, :, pl.ds(0, lead)], xbuf.at[me], load_sem.at[1])
+    mine.start()
+    own = pltpu.make_async_copy(own_ref.at[0], tiles.at[pl.ds(0, slots)], load_sem.at[0])
+    own.start()
     pl.semaphore_wait(barrier, len(peers))
 
     def remote(src, dst, send, recv, to):
@@ -67,8 +70,7 @@
 
     pair = remote(partner_ref.at[0], tiles.at[pl.ds(slots, slots)], pair_s, pair_r, mate)
     pair.start()
-    own = pltpu.make_async_copy(own_ref.at[0], tiles.at[pl.ds(0, slots)], load_sem)
-    own.start()
+    mine.wait()
 
     def slot(dy, zz):
         return xbuf.at[(y + dy) % NY * NZ + zz]
@@ -177,8 +179,8 @@
 
     def list_cols(far_dest, dz, members):
         there = (z + far_dest) % NZ
-        at = (z + dz) % NZ * (NZ // 2) + there // 2
-        return [cols_ref[at, (y + NY - dy) % NY * 2 + child] for dy, child in members]
+        at = (z + dz) % NZ
+        return [cols_ref[there // 2, (child * NY + (y + NY - dy) % NY) * NZ + at] for dy, child in members]
 
     full = [(dy, child) for dy in range(NY) for child in range(2)]
 
@@ -316,7 +318,7 @@
             cell = g * WIDE + n
             block = xbuf[pl.ds(lead // rows + tile // rows * cell, tile // rows)].reshape(tile, lead)
             at = pl.ds(pl.multiple_of(lead + cell * tile, tile), tile)
-            out_ref[0, :, at] = front_ref[0, :, at] - dot3(weights, split(block), NT)
+            out_ref[0, :, at] = -dot3(weights, split(block), NT)
             return carry
 
         lax.fori_loop(0, WIDE, one, 0)
@@ -352,23 +354,31 @@
         for way in range(2):
             raw_start(way, j, False)
 
-    for far in (8, 7, 9, 6, 10, 5, 11):
-        pack(far)
+    def packs(*members):
+        for far in members:
+            pack(far)
+
+    packs(8)
     x_step(1)
+    packs(7, 9)
     wait_y(8)
     for way in range(2):
         raw_start(way, 0, True)
-    for far in (4, 12, 3, 13, 2, 14, 1, 15, 0):
-        pack(far)
+    packs(6, 10)
     x_step(2)
     raw_own(1)
+    packs(5, 11)
     x_step(3)
     raw_forward(1)
+    packs(4, 12)
     x_step(4)
     raw_own(2)
+    packs(3, 13)
     x_step(5)
     raw_forward(2)
+    packs(2, 14)
     x_step(6)
+    packs(1, 15, 0)
     raw_recv(2)
     for way in range(2):
         wait_y(far_of(way, 3))
@@ -450,7 +460,7 @@
     return pl.pallas_call(
         exchange_kernel,
         out_shape=jax.ShapeDtypeStruct(front.shape, f32),
-        in_specs=[vmem, any_spec, any_spec, smem, smem],
+        in_specs=[any_spec, any_spec, any_spec, smem, smem],
         out_specs=vmem,
         scratch_shapes=[
             pltpu.VMEM((2 * slots + 1, tile, tile), f32),
@@ -466,7 +476,7 @@
         + [pltpu.VMEM((lead, lead), bf16)] * 4
         + [pltpu.VMEM((rows, lead), bf16)] * 2
         + [
-            sem, sem, sem,
+            sem((2,)), sem, sem,
             sem((NZ, NY - 1)), sem((NZ, NY - 1)),
             sem((2, 3, 3)), sem((2, 3, 3)),
             sem((2, 5, CHUNKS)), sem((2, 5, CHUNKS)),
@@ -497,10 +507,15 @@
     hit = rows_mine[:, :, None] == jnp.arange(tile_count)
     spot = within[None, :] + slots * jnp.arange(2)[:, None] - 2 * slots
     pick = jnp.sum(jnp.where(hit, spot[:, :, None], 0), axis=1) + 2 * slots
+    rows_here = rows_here.transpose(1, 0, 2)
+    cols_here = cols_here.transpose(1, 0, 2)
     hit = rows_here[None] == (y * (NZ // 2) + jnp.arange(NZ // 2))[:, None, None, None]
     cols = jnp.sum(jnp.where(hit, cols_here - (PANELS - 1), 0), axis=3) - 1
-    cols = cols.reshape(NZ // 2, NY, NZ, 2).transpose(2, 0, 1, 3).reshape(NZ * NZ // 2, 2 * NY)
-    return exchange(front, own_tiles, partner_tiles, pick, cols, PANELS * tile)
+    cols = cols.reshape(NZ // 2, 2 * NY * NZ)
+    lead = PANELS * tile
+    change = exchange(front, own_tiles, partner_tiles, pick, cols, lead)
+    factored = lax.broadcasted_iota(jnp.int32, change.shape, 2) < lead
+    return jnp.where(factored, change, change + front)
 
 
 def solution(mesh):

time: 182 us -> 180 us (0.989)
  local copies, waits for them, and re-layouts: 5.03 us -> 2.44 us
  other arithmetic: 1.62 us -> 3.93 us
    select_n x0 -> x1, other arithmetic: none -> 2.31 us  [body(): return jnp.where(factored, change, change + front)]
    unnamed x3 -> x4, local copies, waits for them, and re-layouts: 3.17 us -> 0.9 us
where the time goes in v6:
time: 180 us
  Pallas kernels  173 us (96%)
  other arithmetic  3.93 us (2%)
  local copies, waits for them, and re-layouts  2.44 us (1%)
    pallas_call x1, Pallas kernels, exchange(): pl.pallas_call(exchange_kernel, out_shape=jax.ShapeDtypeStruct(front.shap...  173 us

profile of v6, /device:TPU:6, one launch (start us, length us, event | category | flops | bytes accessed | tf_op | source)
XLA Modules:
  0.0 179.6 jit_solution(18277380309749859234)
XLA Ops:
  0.0 0.0 copy-start
  0.0 0.9 copy-done
  0.9 0.7 dynamic-slice_bitcast_fusion
  1.6 0.7 dynamic-slice_add_fusion
  2.3 0.1 select_reduce_fusion
  2.4 0.7 sub.28.cols_ref
  3.1 0.2 dynamic-slice_reduce_fusion
  3.3 0.1 add_add_fusion
  3.4 0.1 select_reduce_fusion.1
  3.5 0.6 broadcast_add_fusion.1.pick_ref
  4.1 0.0 copy-start.1
  4.1 173.2 %shard_map.64 = f32[1,64,4096]{2,1,0:T(8,128)} custom-call(f32[1,64,4096]{2,1,0:T(8,128)} %front_ref.1, f32[1,16,128,128]{3,2,1,0:T(8,128)} %own_ref.1, f32[1,16,128,128]{3,2,1,0:T(8,128)} %partner_ref.1, s32[2,32]{1,0:T(2,128)} %broadcast_add_fusion.1.pick_ref, s32[8,128]{1,0:T(8,128)} %sub.28.cols_ref), custom_call_target="tpu_custom_call" | custom-call | tf_op jit(solution)/shard_map/pallas_call | solution.py:460
  177.3 0.0 copy-done.1
  177.3 2.3 %add_select_fusion = f32[1,64,4096]{2,1,0:T(8,128)} fusion(f32[1,64,4096]{2,1,0:T(8,128)} %shard_map.64, f32[1,64,4096]{2,1,0:T(8,128)S(1)} %copy-done.1, pred[4096]{0:T(1024)(128)(4,1)S(1)} %iota_compare_fusion.2), kind=kLoop, calls=%fused_computation | loop fusion | flops 524288 | bytes 3149824 | tf_op jit(solution)/shard_map/jit(_where)/select_n | solution.py:518
  (7 shorter events, 0.0 us)
Async XLA Ops:
  0.0 0.9 copy-start
  4.1 173.2 %copy-start.1 = (f32[1,64,4096]{2,1,0:T(8,128)S(1)}, f32[1,64,4096]{2,1,0:T(8,128)}, u32[]{:S(2)}) copy-start(f32[1,64,4096]{2,1,0:T(8,128)} %front_ref.1) | copy-start | bytes 3145732

commit v7 on v6

--- a/solution.py
+++ b/solution.py
@@ -33,10 +33,32 @@
     return small + dot1(left[0], right[0], dims)
 
 
+def fill_table(table, rows_ref, cols_ref, live_ref, side, y, me, slots):
+    devices = rows_ref.shape[2]
+    table[...] = jnp.zeros(table.shape, jnp.int32)
+    spot = lax.broadcasted_iota(jnp.int32, (slots, devices), 0)
+    lane = lax.broadcasted_iota(jnp.int32, (slots, devices), 1)
+    wide_spot = lax.broadcasted_iota(jnp.int32, (slots, 128), 0)
+    wide_lane = lax.broadcasted_iota(jnp.int32, (slots, 128), 1)
+    for child in range(2):
+        at = pl.ds(child * slots, slots)
+        alive = spot < live_ref[side, pl.ds(child, 1), :]
+        rows = jnp.where(alive, rows_ref[side, at, :], -1)
+        cells = cols_ref[side, at, :] - (PANELS - 1)
+        for q in range(NZ // 2):
+            hit = rows == y * (NZ // 2) + q
+            found = jnp.sum(jnp.where(hit, cells, 0), axis=0, keepdims=True) - 1
+            table[pl.ds(2 * q + child, 1), pl.ds(0, devices)] = found
+        mine = jnp.sum(jnp.where(lane == me, rows, 0), axis=1, keepdims=True)
+        slot = wide_spot + (child * slots - 2 * slots)
+        found = jnp.sum(jnp.where(mine == wide_lane, slot, 0), axis=0, keepdims=True)
+        table[pl.ds(NZ + child, 1), :] = found + 2 * slots
+
+
 def exchange_kernel(
-    front_ref, own_ref, partner_ref, pick_ref, cols_ref, out_ref,
+    front_ref, own_ref, partner_ref, rows_ref, cols_ref, live_ref, out_ref,
     tiles, packed, ybuf, raw1, raw2, raw3, dense, xbuf,
-    lead_ref, m_ref, t_ref, g_ref, a_hi, a_lo, m_hi, m_lo, w_hi, w_lo,
+    table, plan, lead_ref, m_ref, t_ref, g_ref, a_hi, a_lo, m_hi, m_lo, w_hi, w_lo,
     load_sem, pair_s, pair_r, y_s, y_r, raw_s, raw_r, d_s, d_r,
     zr_s, zr_r, zl_s, zl_r, yp_s, yp_r, ym_s, ym_r, fp_s, fp_r, fm_s, fm_r,
 ):
@@ -61,6 +83,9 @@
     mine.start()
     own = pltpu.make_async_copy(own_ref.at[0], tiles.at[pl.ds(0, slots)], load_sem.at[0])
     own.start()
+    fill_table(table, rows_ref, cols_ref, live_ref, side, y, me, slots)
+    planned = pltpu.make_async_copy(table, plan, load_sem.at[2])
+    planned.start()
     pl.semaphore_wait(barrier, len(peers))
 
     def remote(src, dst, send, recv, to):
@@ -120,6 +145,7 @@
     x_right(0).start()
     x_left(0).start()
     tiles[none] = jnp.zeros(tiles.shape[1:], jnp.float32)
+    planned.wait()
     own.wait()
     pair.wait()
 
@@ -134,7 +160,7 @@
         top = pl.multiple_of(there % 2 * rows, rows)
         for to_y in range(NY):
             for child in range(2):
-                index = pick_ref[child, to_y * (NZ // 2) + there // 2]
+                index = plan[NZ + child, to_y * (NZ // 2) + there // 2]
                 packed[far, to_y, child] = tiles[index, pl.ds(top, rows), :]
         for dy in range(1, NY):
             over_y(far, dy).start()
@@ -180,7 +206,7 @@
     def list_cols(far_dest, dz, members):
         there = (z + far_dest) % NZ
         at = (z + dz) % NZ
-        return [cols_ref[there // 2, (child * NY + (y + NY - dy) % NY) * NZ + at] for dy, child in members]
+        return [plan[there // 2 * 2 + child, (y + NY - dy) % NY * NZ + at] for dy, child in members]
 
     full = [(dy, child) for dy in range(NY) for child in range(2)]
 
@@ -448,19 +474,18 @@
                 go(way, j, g).wait_send()
 
 
-def exchange(front, own_tiles, partner_tiles, pick, cols, lead):
+def exchange(front, own_tiles, partner_tiles, tile_rows, tile_cols, live, lead):
     rows = front.shape[1]
     tile = own_tiles.shape[-1]
     slots = own_tiles.shape[1]
     sem = pltpu.SemaphoreType.DMA
     any_spec = pl.BlockSpec(memory_space=pl.ANY)
-    smem = pl.BlockSpec(memory_space=pltpu.SMEM)
     vmem = pl.BlockSpec(memory_space=pltpu.VMEM)
     f32, bf16 = jnp.float32, jnp.bfloat16
     return pl.pallas_call(
         exchange_kernel,
         out_shape=jax.ShapeDtypeStruct(front.shape, f32),
-        in_specs=[any_spec, any_spec, any_spec, smem, smem],
+        in_specs=[any_spec, any_spec, any_spec, vmem, vmem, vmem],
         out_specs=vmem,
         scratch_shapes=[
             pltpu.VMEM((2 * slots + 1, tile, tile), f32),
@@ -472,11 +497,12 @@
             pltpu.VMEM((2, 6, CELLS, rows, tile), f32),
             pltpu.VMEM((NY * NZ, rows, lead), f32),
         ]
+        + [pltpu.VMEM((24, 128), jnp.int32), pltpu.SMEM((24, 128), jnp.int32)]
         + [pltpu.VMEM((lead, lead), f32)] * 4
         + [pltpu.VMEM((lead, lead), bf16)] * 4
         + [pltpu.VMEM((rows, lead), bf16)] * 2
         + [
-            sem((2,)), sem, sem,
+            sem((3,)), sem, sem,
             sem((NZ, NY - 1)), sem((NZ, NY - 1)),
             sem((2, 3, 3)), sem((2, 3, 3)),
             sem((2, 5, CHUNKS)), sem((2, 5, CHUNKS)),
@@ -485,35 +511,15 @@
         compiler_params=pltpu.CompilerParams(
             collective_id=0, has_side_effects=True, vmem_limit_bytes=56 * 2**20
         ),
-    )(front, own_tiles, partner_tiles, pick, cols)
+    )(front, own_tiles, partner_tiles, tile_rows, tile_cols, live)
 
 
 def body(front, own_tiles, partner_tiles, tile_rows, tile_cols, live):
-    position = lax.axis_index("cube")
-    front_pos = lax.axis_index("front")
-    tile = own_tiles.shape[-1]
-    slots = own_tiles.shape[1]
-    tile_count = front.shape[2] // tile
-    y, z = position // NZ, position % NZ
-
-    rows_here = lax.dynamic_index_in_dim(tile_rows, front_pos, 0, keepdims=False)[:, :, 0]
-    cols_here = lax.dynamic_index_in_dim(tile_cols, front_pos, 0, keepdims=False)
-    live_here = lax.dynamic_index_in_dim(live, front_pos, 0, keepdims=False)
-    within = jnp.arange(slots)
-    rows_here = rows_here.reshape(NY * NZ, 2, slots)
-    cols_here = cols_here.reshape(NY * NZ, 2, slots)
-    rows_here = jnp.where(within < live_here[:, :, None], rows_here, -1)
-    rows_mine = lax.dynamic_index_in_dim(rows_here, position, 0, keepdims=False)
-    hit = rows_mine[:, :, None] == jnp.arange(tile_count)
-    spot = within[None, :] + slots * jnp.arange(2)[:, None] - 2 * slots
-    pick = jnp.sum(jnp.where(hit, spot[:, :, None], 0), axis=1) + 2 * slots
-    rows_here = rows_here.transpose(1, 0, 2)
-    cols_here = cols_here.transpose(1, 0, 2)
-    hit = rows_here[None] == (y * (NZ // 2) + jnp.arange(NZ // 2))[:, None, None, None]
-    cols = jnp.sum(jnp.where(hit, cols_here - (PANELS - 1), 0), axis=3) - 1
-    cols = cols.reshape(NZ // 2, 2 * NY * NZ)
-    lead = PANELS * tile
-    change = exchange(front, own_tiles, partner_tiles, pick, cols, lead)
+    lead = PANELS * own_tiles.shape[-1]
+    tile_rows = tile_rows[:, :, :, 0].transpose(0, 2, 1)
+    tile_cols = tile_cols.transpose(0, 2, 1)
+    live = live.transpose(0, 2, 1)
+    change = exchange(front, own_tiles, partner_tiles, tile_rows, tile_cols, live, lead)
     factored = lax.broadcasted_iota(jnp.int32, change.shape, 2) < lead
     return jnp.where(factored, change, change + front)
 

time: 180 us -> 176 us (0.978)
  local copies, waits for them, and re-layouts: 2.44 us -> 0.01 us
where the time goes in v7:
time: 176 us
  Pallas kernels  173 us (98%)
  other arithmetic  2.31 us (1%)
    pallas_call x1, Pallas kernels, exchange(): pl.pallas_call(exchange_kernel, out_shape=jax.ShapeDtypeStruct(front.shap...  173 us

profile of v7, /device:TPU:6, one launch (start us, length us, event | category | flops | bytes accessed | tf_op | source)
XLA Modules:
  0.0 175.7 jit_solution(8515214526680255948)
XLA Ops:
  0.0 0.0 copy-start
  0.0 173.4 %shard_map.64 = f32[1,64,4096]{2,1,0:T(8,128)} custom-call(f32[1,64,4096]{2,1,0:T(8,128)} %front_ref.1, f32[1,16,128,128]{3,2,1,0:T(8,128)} %own_ref.1, f32[1,16,128,128]{3,2,1,0:T(8,128)} %partner_ref.1, s32[8,32,64]{2,1,0:T(8,128)} %bitcast.5, s32[8,32,64]{2,1,0:T(8,128)} %bitcast.6, s32[8,2,64]{2,1,0:T(2,128)} %bitcast.7), custom_call_target="tpu_custom_call" | custom-call | tf_op jit(solution)/shard_map/pallas_call | solution.py:485
  173.4 0.0 copy-done
  173.4 2.3 %add_select_fusion = f32[1,64,4096]{2,1,0:T(8,128)} fusion(f32[1,64,4096]{2,1,0:T(8,128)} %shard_map.64, f32[1,64,4096]{2,1,0:T(8,128)S(1)} %copy-done, pred[4096]{0:T(1024)(128)(4,1)S(1)} %iota_compare_fusion), kind=kLoop, calls=%fused_computation | loop fusion | flops 524288 | bytes 3149824 | tf_op jit(solution)/shard_map/jit(_where)/select_n | solution.py:524
  (1 shorter events, 0.0 us)
Async XLA Ops:
  0.0 173.4 %copy-start = (f32[1,64,4096]{2,1,0:T(8,128)S(1)}, f32[1,64,4096]{2,1,0:T(8,128)}, u32[]{:S(2)}) copy-start(f32[1,64,4096]{2,1,0:T(8,128)} %front_ref.1) | copy-start | bytes 3145732

commit v8 on v7

--- a/solution.py
+++ b/solution.py
@@ -146,6 +146,7 @@
     x_left(0).start()
     tiles[none] = jnp.zeros(tiles.shape[1:], jnp.float32)
     planned.wait()
+    x_step(1)
     own.wait()
     pair.wait()
 
@@ -365,18 +366,15 @@
         for copy in copies[:count] if own else copies[count:]:
             copy.start()
 
-    def raw_recv(j):
-        for way in range(2):
-            for copy in raw_go(way, j):
-                copy.wait_recv()
-
     def raw_own(j):
         for way in range(2):
             wait_y(far_of(way, j))
             raw_start(way, j, True)
 
     def raw_forward(j):
-        raw_recv(j - 1)
+        for way in range(2):
+            for copy in raw_go(way, j - 1):
+                copy.wait_recv()
         for way in range(2):
             raw_start(way, j, False)
 
@@ -384,40 +382,45 @@
         for far in members:
             pack(far)
 
-    packs(8)
-    x_step(1)
-    packs(7, 9)
+    packs(8, 7, 9)
+    x_step(2)
     wait_y(8)
     for way in range(2):
         raw_start(way, 0, True)
     packs(6, 10)
-    x_step(2)
+    x_step(3)
     raw_own(1)
     packs(5, 11)
-    x_step(3)
+    x_step(4)
     raw_forward(1)
     packs(4, 12)
-    x_step(4)
+    x_step(5)
     raw_own(2)
     packs(3, 13)
-    x_step(5)
+    x_step(6)
     raw_forward(2)
-    packs(2, 14)
-    x_step(6)
-    packs(1, 15, 0)
-    raw_recv(2)
+    packs(2, 14, 1, 15, 0)
+    later = []
     for way in range(2):
-        wait_y(far_of(way, 3))
-    items = [own_items(far_of(way, 3)) + raw_items(way, far_of(way, 3)) for way in range(2)]
+        far = far_of(way, 3)
+        wait_y(far)
+        for copy in raw_go(way, 2)[:2]:
+            copy.wait_recv()
+        lists = raw_items(way, far)
+        later.append(lists[8:])
+        for g in range(CHUNKS):
+            merge(dense.at[way, 0], True, own_items(far) + lists[:8], g)
+    x_step(7)
+    for way in range(2):
+        raw_go(way, 2)[2].wait_recv()
     for g in range(CHUNKS):
         for way in range(2):
-            merge(dense.at[way, 0], True, items[way], g)
+            merge(dense.at[way, 0], False, later[way], g)
             go(way, 3, g).start()
         if g == 1:
-            x_step(7)
-    x_step(8)
-    for zz in range(8):
-        x_out(zz)
+            x_step(8)
+            for zz in range(8):
+                x_out(zz)
     outs, passes = list(range(8, NZ)), list(range(NZ))
     for j in range(4, 8):
         for way in range(2):
@@ -429,15 +432,14 @@
                 merge(dense.at[way, j - 3], False, items[way], g)
                 go(way, j, g).start()
             slot_at = (j - 4) * CHUNKS + g
-            if slot_at > 0:
-                for zz in passes[:2]:
-                    x_pass(zz)
-                del passes[:2]
-                for zz in outs[:2]:
-                    x_out(zz)
-                del outs[:2]
-            if slot_at > 5:
-                work(2 if slot_at < 12 else 3)
+            for zz in passes[:2]:
+                x_pass(zz)
+            del passes[:2]
+            for zz in outs[:2]:
+                x_out(zz)
+            del outs[:2]
+            if slot_at > 4:
+                work(2 if slot_at < 14 else 3)
 
     while todo:
         work(1)

time: 176 us -> 170 us (0.966)
  Pallas kernels: 173 us -> 168 us
    pallas_call x1, Pallas kernels: 173 us -> 168 us  [exchange(): pl.pallas_call(exchange_kernel, out_shape=jax.ShapeDtypeStruct(front.shap...]
where the time goes in v8:
time: 170 us
  Pallas kernels  168 us (99%)
  other arithmetic  2.31 us (1%)
    pallas_call x1, Pallas kernels, exchange(): pl.pallas_call(exchange_kernel, out_shape=jax.ShapeDtypeStruct(front.shap...  168 us

profile of v8, /device:TPU:6, one launch (start us, length us, event | category | flops | bytes accessed | tf_op | source)
XLA Modules:
  0.0 170.1 jit_solution(12054784498937411415)
XLA Ops:
  0.0 0.0 copy-start
  0.0 167.8 %shard_map.64 = f32[1,64,4096]{2,1,0:T(8,128)} custom-call(f32[1,64,4096]{2,1,0:T(8,128)} %front_ref.1, f32[1,16,128,128]{3,2,1,0:T(8,128)} %own_ref.1, f32[1,16,128,128]{3,2,1,0:T(8,128)} %partner_ref.1, s32[8,32,64]{2,1,0:T(8,128)} %bitcast.5, s32[8,32,64]{2,1,0:T(8,128)} %bitcast.6, s32[8,2,64]{2,1,0:T(2,128)} %bitcast.7), custom_call_target="tpu_custom_call" | custom-call | tf_op jit(solution)/shard_map/pallas_call | solution.py:487
  167.8 0.0 copy-done
  167.8 2.3 %add_select_fusion = f32[1,64,4096]{2,1,0:T(8,128)} fusion(f32[1,64,4096]{2,1,0:T(8,128)} %shard_map.64, f32[1,64,4096]{2,1,0:T(8,128)S(1)} %copy-done, pred[4096]{0:T(1024)(128)(4,1)S(1)} %iota_compare_fusion), kind=kLoop, calls=%fused_computation | loop fusion | flops 524288 | bytes 3149824 | tf_op jit(solution)/shard_map/jit(_where)/select_n | solution.py:526
  (1 shorter events, 0.0 us)
Async XLA Ops:
  0.0 167.8 %copy-start = (f32[1,64,4096]{2,1,0:T(8,128)S(1)}, f32[1,64,4096]{2,1,0:T(8,128)}, u32[]{:S(2)}) copy-start(f32[1,64,4096]{2,1,0:T(8,128)} %front_ref.1) | copy-start | bytes 3145732

commit v9 on v8

--- a/solution.py
+++ b/solution.py
@@ -382,8 +382,9 @@
         for far in members:
             pack(far)
 
-    packs(8, 7, 9)
+    packs(8)
     x_step(2)
+    packs(7, 9)
     wait_y(8)
     for way in range(2):
         raw_start(way, 0, True)

time: 170 us -> 173 us (1.018)
  Pallas kernels: 168 us -> 170 us
    pallas_call x1, Pallas kernels: 168 us -> 170 us  [exchange(): pl.pallas_call(exchange_kernel, out_shape=jax.ShapeDtypeStruct(front.shap...]
where the time goes in v9:
time: 173 us
  Pallas kernels  170 us (98%)
  other arithmetic  2.31 us (1%)
    pallas_call x1, Pallas kernels, exchange(): pl.pallas_call(exchange_kernel, out_shape=jax.ShapeDtypeStruct(front.shap...  170 us

profile of v9, /device:TPU:6, one launch (start us, length us, event | category | flops | bytes accessed | tf_op | source)
XLA Modules:
  0.0 172.8 jit_solution(10676343347500346545)
XLA Ops:
  0.0 0.0 copy-start
  0.0 170.4 %shard_map.64 = f32[1,64,4096]{2,1,0:T(8,128)} custom-call(f32[1,64,4096]{2,1,0:T(8,128)} %front_ref.1, f32[1,16,128,128]{3,2,1,0:T(8,128)} %own_ref.1, f32[1,16,128,128]{3,2,1,0:T(8,128)} %partner_ref.1, s32[8,32,64]{2,1,0:T(8,128)} %bitcast.5, s32[8,32,64]{2,1,0:T(8,128)} %bitcast.6, s32[8,2,64]{2,1,0:T(2,128)} %bitcast.7), custom_call_target="tpu_custom_call" | custom-call | tf_op jit(solution)/shard_map/pallas_call | solution.py:488
  170.4 0.0 copy-done
  170.5 2.3 %add_select_fusion = f32[1,64,4096]{2,1,0:T(8,128)} fusion(f32[1,64,4096]{2,1,0:T(8,128)} %shard_map.64, f32[1,64,4096]{2,1,0:T(8,128)S(1)} %copy-done, pred[4096]{0:T(1024)(128)(4,1)S(1)} %iota_compare_fusion), kind=kLoop, calls=%fused_computation | loop fusion | flops 524288 | bytes 3149824 | tf_op jit(solution)/shard_map/jit(_where)/select_n | solution.py:527
  (1 shorter events, 0.0 us)
Async XLA Ops:
  0.0 170.4 %copy-start = (f32[1,64,4096]{2,1,0:T(8,128)S(1)}, f32[1,64,4096]{2,1,0:T(8,128)}, u32[]{:S(2)}) copy-start(f32[1,64,4096]{2,1,0:T(8,128)} %front_ref.1) | copy-start | bytes 3145732
